TPU v7x, 256 devices: a whole 4x4x8 slice. The times are simulated.
256 devices in a mesh: member: 4 (over y_hi, core), node: 64 (over y_lo, x, z).
Axes of the slice: x: 4, y: 4 (y_hi: 2, y_lo: 2; y = y_hi * 2 + y_lo), z: 8, core: 2. Of those that a mesh axis runs over, the one named last changes fastest.
Arguments:
- gridpoint_state: bfloat16 [218, 65536], P(None, 'node'), may hold values from -6 to 6
- grid_truth: bfloat16 [100, 65536], P(None, 'node'), may hold values from -6 to 6
- encoder_slots: int32 [16384, 16], P('node'), may hold values from 0 to 65535, as said below
- encoder_count: int32 [16384], P('node'), may hold values from 1 to 16
- node_reach: int32 [16384], P('node'), may hold values from 128 to 256
- decoder_slots: int32 [65536, 4], P('node'), may hold values from 0 to 16383, as said below
- member_perturb: bfloat16 [4, 16384, 1024], P('member', 'node'), may hold values from -6 to 6
- embed_weight: bfloat16 [218, 1024], replicated, may hold values from -0.4375 to 0.4375
- norm_gains: float32 [3, 1024], replicated, may hold values from 0.1 to 1.9
- qkv_weight: bfloat16 [1024, 3072], replicated
- out_weight: bfloat16 [1024, 1024], replicated, may hold values from -0.1875 to 0.1875
- up_weight: bfloat16 [1024, 4096], P('node'), may hold values from -0.1875 to 0.1875
- down_weight: bfloat16 [1024, 4096], P('node'), may hold values from -0.09375 to 0.09375
- head_weight: bfloat16 [1024, 100], replicated, may hold values from -0.1875 to 0.1875
Outputs:
- crps_grad: float32 [4, 100, 65536], P('member', None, 'node')
Inputs may be any that keep to these rules, and one draw needn't show every extreme that they name: `encoder_slots`: for a hidden node of region r (nodes r * 256 to (r + 1) * 256 - 1), every slot names a grid point of region r - 1, r or r + 1, a region holding 1024 consecutive points; slots from encoder_count on are padding. `decoder_slots`: for a grid point of region r, every slot names a hidden node of region r - 1, r or r + 1.
All inputs are finite; a program needn't handle non-finite values.
Results may differ from a plain program's by a relative error of at most 0.0095.
The roundings to bfloat16 on the way count: a program that leaves them out, or rounds other values in their place, can miss the bound.
Values may be sent and summed in bfloat16 or wider, within the bound.
No kernel may reach another device: no remote copies, remote signals or barrier semaphores. Data moves between devices by JAX's collectives and lax.ppermute only.
A program may use at most 128 MiB of HBM per device.

v0:
```python
import jax
import jax.numpy as jnp
from jax import lax
from jax.sharding import Mesh
from jax.sharding import PartitionSpec as P

HEADS = 16
HEAD_DIM = 64
BAND = 256
NODE = ("node_0", "node_1", "node_2")


EPS = 1e-05
SMOOTH = 0.25


def with_halo(block, sides, width):
    for axis, dim in sides:
        count = lax.axis_size(axis)
        forward = [(i, i + 1) for i in range(count - 1)]
        backward = [(target, source) for source, target in forward]
        low = lax.ppermute(
            lax.slice_in_dim(block, block.shape[dim] - width, None, axis=dim), axis, forward
        )
        high = lax.ppermute(lax.slice_in_dim(block, 0, width, axis=dim), axis, backward)
        block = jnp.concatenate([low, block, high], axis=dim)
    return block


def in_order(blocks, dim):
    blocks = jnp.moveaxis(blocks, 0, dim)
    dims = blocks.shape
    return blocks.reshape(*dims[:dim], dims[dim] * dims[dim + 1], *dims[dim + 2 :])


def gather_in_order(shard, axes, sequence):
    blocks = shard[None]
    for k in sequence:
        blocks = lax.all_gather(blocks, axes[k], axis=0, tiled=True)
    current = [lax.axis_size(axes[k]) for k in reversed(sequence)]
    blocks = blocks.reshape(*current, *shard.shape)
    turned = sorted(range(len(sequence)), key=lambda place: sequence[len(sequence) - 1 - place])
    return blocks.transpose(*turned, *range(len(sequence), blocks.ndim)).reshape(-1, *shard.shape)


def gathered_by_axis(shard, axes, sequence, dim):
    return in_order(gather_in_order(shard, axes, sequence), dim)


def layer_norm(entries, scale_gain):
    average = jnp.mean(entries, axis=-1, keepdims=True)
    centred = entries - average
    variance = jnp.mean(centred * centred, axis=-1, keepdims=True)
    return centred * lax.rsqrt(variance + EPS) * scale_gain


def score_gradient(difference):
    return difference * lax.rsqrt(difference * difference + SMOOTH * SMOOTH)


def times_rows(left_side, right_side):
    return lax.dot_general(
        left_side, right_side, (((1,), (1,)), ((), ())), preferred_element_type=jnp.float32
    )


def banded_attention(query_rows, bordered, first_query, first_key, node_total, reaches):
    query_count = query_rows.shape[0]
    key_count = bordered.shape[0]
    model_width = query_rows.shape[1]
    key_heads = bordered[:, :model_width].reshape(key_count, HEADS, HEAD_DIM)
    value_heads = bordered[:, model_width:].reshape(key_count, HEADS, HEAD_DIM)
    queries = query_rows.reshape(query_count, HEADS, HEAD_DIM)
    scores = jnp.einsum(
        "qhd,khd->hqk", queries, key_heads, preferred_element_type=jnp.float32
    ) * HEAD_DIM ** (-0.5)
    rows_at = first_query + jnp.arange(query_count, dtype=jnp.int32)
    cols_at = first_key + jnp.arange(key_count, dtype=jnp.int32)
    distance = jnp.abs(rows_at[:, None] - cols_at[None, :])
    allowed = (
        (distance <= reaches[:, None]) & (cols_at[None, :] >= 0) & (cols_at[None, :] < node_total)
    )
    masked = jnp.where(allowed[None], scores, -1e30)
    highest = jnp.max(masked, axis=-1, keepdims=True)
    weights = jnp.where(allowed[None], jnp.exp(masked - highest), 0.0)
    chances = (weights / jnp.sum(weights, axis=-1, keepdims=True)).astype(jnp.bfloat16)
    blended = jnp.einsum("hqk,khd->qhd", chances, value_heads, preferred_element_type=jnp.float32)
    return blended.reshape(query_count, model_width).astype(jnp.bfloat16)


def per_device(
    gridpoint_state,
    grid_truth,
    encoder_slots,
    encoder_count,
    node_reach,
    decoder_slots,
    member_perturb,
    embed_weight,
    norm_gains,
    qkv_weight,
    out_weight,
    up_weight,
    down_weight,
    head_weight,
):
    region = lax.axis_index(NODE)
    region_count = lax.axis_size(NODE)
    ensemble_size = lax.axis_size("member")
    member_index = lax.axis_index("member")
    grid_dev = gridpoint_state.shape[1]
    node_dev = encoder_slots.shape[0]
    model_width = embed_weight.shape[1]
    node_total = node_dev * region_count
    widened = with_halo(gridpoint_state, ((NODE, 1),), grid_dev)
    local_slots = encoder_slots - (region - 1) * grid_dev
    window = jnp.arange(3 * grid_dev, dtype=jnp.int32)
    tallies = jnp.zeros((node_dev, 3 * grid_dev), jnp.float32)
    for position in range(encoder_slots.shape[1]):
        live = position < encoder_count
        hits = (local_slots[:, position][:, None] == window[None, :]) & live[:, None]
        tallies = tallies + hits.astype(jnp.float32)
    pooled_sum = times_rows(tallies.astype(jnp.bfloat16), widened)
    pooled_nodes = (pooled_sum / encoder_count[:, None].astype(jnp.float32)).astype(jnp.bfloat16)
    embedded = jnp.dot(pooled_nodes, embed_weight, preferred_element_type=jnp.float32)
    hidden_start = embedded + member_perturb[0].astype(jnp.float32)
    normed = layer_norm(hidden_start, norm_gains[0]).astype(jnp.bfloat16)
    project = jnp.dot(normed, qkv_weight, preferred_element_type=jnp.float32).astype(jnp.bfloat16)
    query_rows = project[:, :model_width]
    bordered = with_halo(project[:, model_width:], ((NODE, 0),), BAND)
    first_query = region * node_dev
    attended = banded_attention(
        query_rows, bordered, first_query, first_query - BAND, node_total, node_reach
    )
    hidden_mid = hidden_start + jnp.dot(attended, out_weight, preferred_element_type=jnp.float32)
    normed_mid = layer_norm(hidden_mid, norm_gains[1]).astype(jnp.bfloat16)
    up_whole = gathered_by_axis(up_weight, NODE, (0, 1, 2), 0)
    upper = jnp.dot(normed_mid, up_whole, preferred_element_type=jnp.float32)
    active = jax.nn.gelu(upper).astype(jnp.bfloat16)
    down_whole = gathered_by_axis(down_weight, NODE, (0, 1, 2), 0)
    lowered = times_rows(active, down_whole)
    final = layer_norm(hidden_mid + lowered, norm_gains[2]).astype(jnp.bfloat16)
    local_nodes = decoder_slots - (region - 1) * node_dev
    variable_count = head_weight.shape[1]
    slot_count = decoder_slots.shape[1]
    projected = lax.dot_general(
        head_weight, final, (((0,), (1,)), ((), ())), preferred_element_type=jnp.float32
    )
    projected_near = with_halo(projected.astype(jnp.bfloat16), ((NODE, 1),), node_dev).astype(
        projected.dtype
    )
    summed = jnp.zeros((variable_count, grid_dev), jnp.float32)
    for position in range(slot_count):
        summed = summed + jnp.take(projected_near, local_nodes[:, position], axis=1)
    state_delta = summed / slot_count
    predicted_field = gridpoint_state[:variable_count].astype(jnp.float32) + state_delta
    pairwise_scale = 1.0 / (ensemble_size * (ensemble_size - 1))
    share = grid_dev // ensemble_size
    mine = lax.all_to_all(predicted_field[None], "member", split_axis=2, concat_axis=0, tiled=True)
    observed_field = lax.dynamic_slice_in_dim(grid_truth, member_index * share, share, 1).astype(
        jnp.float32
    )
    pairwise_sum = jnp.zeros_like(mine)
    for other_member in range(ensemble_size):
        pairwise_sum = pairwise_sum + score_gradient(mine - mine[other_member][None])
    gradients = (
        score_gradient(mine - observed_field[None]) / ensemble_size - pairwise_sum * pairwise_scale
    )
    return lax.all_to_all(
        gradients.astype(jnp.bfloat16), "member", split_axis=0, concat_axis=2, tiled=True
    ).astype(gradients.dtype)


def solution(mesh):
    torus = Mesh(
        mesh.devices.reshape(mesh.shape["member"], 2, 4, 8),
        ("member", "node_0", "node_1", "node_2"),
    )
    return jax.shard_map(
        per_device,
        mesh=torus,
        in_specs=(
            P(None, NODE),
            P(None, NODE),
            P(NODE, None),
            P(NODE),
            P(NODE),
            P(NODE, None),
            P("member", NODE, None),
            P(),
            P(),
            P(),
            P(),
            P(NODE, None),
            P(NODE, None),
            P(),
        ),
        out_specs=P("member", None, NODE),
        check_vma=False,
    )
```

profile of v0, /device:TPU:8, one launch (start us, length us, event | category | flops | bytes accessed | tf_op | source)
XLA Modules:
  0.0 375.4 jit_solution(6813843629020049477)
XLA Ops:
  6.6 0.0 all-gather.11.cloned.1.call-start
  6.6 7.8 %all-gather.1 = bf16[32,4096]{1,0:T(8,128)(2,1)} all-gather(bf16[16,4096]{1,0:T(8,128)(2,1)} %param.28), channel_id=3, replica_groups=mesh['member'=4,'node_0'=2,'node_1'=4,'node_2'=8] {'node_0'}, dimensions={0}, use_global_device_ids=true | all-gather | bytes 393216 | tf_op jit(solution)/shard_map/all_gather | solution.py:39
  14.4 0.0 all-gather.11.cloned.1.call-update
  14.4 0.0 all-gather.7.cloned.1.call-start
  14.5 6.0 %all-gather = bf16[32,4096]{1,0:T(8,128)(2,1)} all-gather(bf16[16,4096]{1,0:T(8,128)(2,1)} %param.27), channel_id=2, replica_groups=mesh['member'=4,'node_0'=2,'node_1'=4,'node_2'=8] {'node_0'}, dimensions={0}, use_global_device_ids=true | all-gather | bytes 393216 | tf_op jit(solution)/shard_map/all_gather | solution.py:39
  20.4 0.0 all-gather.7.cloned.1.call-update
  20.5 0.0 all-gather.13.cloned.1.call-start
  20.5 23.1 %all-gather.11.cloned.1.call-done = bf16[8,16,4096]{2,1,0:T(8,128)(2,1)} async-done(((bf16[2,16,4096]{2,1,0:T(8,128)(2,1)}), bf16[8,16,4096]{2,1,0:T(8,128)(2,1)}) %all-gather.11.cloned.1.call-update) | async-done | bytes 1048592 | tf_op jit(solution)/shard_map/all_gather | solution.py:39
  43.6 0.0 all-gather.13.cloned.1.call-update
  43.6 0.0 all-gather.9.cloned.1.call-start
  43.7 28.6 %all-gather.7.cloned.1.call-done = bf16[8,16,4096]{2,1,0:T(8,128)(2,1)} async-done(((bf16[2,16,4096]{2,1,0:T(8,128)(2,1)}), bf16[8,16,4096]{2,1,0:T(8,128)(2,1)}) %all-gather.7.cloned.1.call-update) | async-done | bytes 1048592 | tf_op jit(solution)/shard_map/all_gather | solution.py:39
  72.3 0.0 all-gather.9.cloned.1.call-update
  72.3 6.4 %collective-permute-start.1 = (bf16[218,1024]{1,0:T(8,128)(2,1)S(1)}, bf16[218,1024]{1,0:T(8,128)(2,1)S(1)}, u32[]{:S(2)}, u32[]{:S(2)}) collective-permute-start(bf16[218,1024]{1,0:T(8,128)(2,1)S(1)} %copy-done.4), channel_id=1, source_target_pairs={{1,0},{2,1},{3,2},{4,3},{5,4},{6,5},{7,6},{8,7},{9,8},{10,9},{11,1... | collective-permute-start | bytes 1339400 | tf_op jit(solution)/shard_map/ppermute | solution.py:25
  78.8 1.9 collective-permute-start
  80.9 9.8 %collective-permute-done.1 = bf16[218,1024]{1,0:T(8,128)(2,1)S(1)} collective-permute-done((bf16[218,1024]{1,0:T(8,128)(2,1)S(1)}, bf16[218,1024]{1,0:T(8,128)(2,1)S(1)}, u32[]{:S(2)}, u32[]{:S(2)}) %collective-permute-start.1) | collective-permute-done | bytes 446496 | tf_op jit(solution)/shard_map/ppermute | solution.py:25
  90.7 11.8 %collective-permute-done = bf16[218,1024]{1,0:T(8,128)(2,1)} collective-permute-done((bf16[218,1024]{1,0:T(8,128)(2,1)S(1)}, bf16[218,1024]{1,0:T(8,128)(2,1)}, u32[]{:S(2)}, u32[]{:S(2)}) %collective-permute-start) | collective-permute-done | bytes 446496 | tf_op jit(solution)/shard_map/ppermute | solution.py:22
  102.5 12.2 %fusion.125 = (f32[256]{0:T(256)S(1)}, f32[256,1024]{1,0:T(8,128)S(1)}) fusion(bf16[1,256,1024]{2,1,0:T(8,128)(2,1)} %param.22, bf16[218,1024]{1,0:T(8,128)(2,1)} %param.23, bf16[218,1024]{1,0:T(8,128)(2,1)} %copy-done.12, bf16[218,1024]{1,0:T(8,128)(2,1)} %param.16, bf16[218,1024]{1,0:T(8,128)(2,1)} %collective-permute-done, s32[256]{0:T(256)S(1)} %bitcast.132, ...), kind=kOutput, calls=%fused_computation.198 | convolution fusion | flops 512426752 | bytes 3381248 | tf_op jit(solution)/shard_map/dot_general | solution.py:125
  114.7 0.3 multiply_reduce_fusion.2
  115.0 5.0 %convolution_convert_fusion = bf16[256,3072]{1,0:T(8,128)(2,1)S(1)} fusion(bf16[1024,3072]{1,0:T(8,128)(2,1)} %param.25, f32[256,1024]{1,0:T(8,128)S(1)} %get-tuple-element.52, f32[1024]{0:T(1024)S(1)} %bitcast.130, f32[256]{0:T(256)S(1)} %add_rsqrt_fusion.2, f32[256]{0:T(256)S(1)} %broadcast_multiply_fusion.2), kind=kOutput, calls=%fused_computation.22 | convolution fusion | flops 1612447744 | bytes 8919040 | tf_op jit(solution)/shard_map/dot_general | solution.py:128
  119.9 1.1 slice.157
  121.1 1.9 collective-permute-start.3
  123.0 3.9 %collective-permute-start.2 = (bf16[256,2048]{1,0:T(8,128)(2,1)}, bf16[256,2048]{1,0:T(8,128)(2,1)}, u32[]{:S(2)}, u32[]{:S(2)}) collective-permute-start(bf16[256,2048]{1,0:T(8,128)(2,1)} %slice.157), channel_id=1, source_target_pairs={{0,1},{1,2},{2,3},{3,4},{4,5},{5,6},{6,7},{7,8},{8,9},{9,10},{10,1... | collective-permute-start | bytes 3145736 | tf_op jit(solution)/shard_map/ppermute | solution.py:22
  127.0 0.6 compare_and_fusion
  127.5 0.6 compare_and_fusion.2
  128.1 0.3 fusion.90
  128.5 0.8 slice.159
  129.3 2.0 copy.61
  131.4 37.4 %collective-permute-done.3 = bf16[256,2048]{1,0:T(8,128)(2,1)} collective-permute-done((bf16[256,2048]{1,0:T(8,128)(2,1)}, bf16[256,2048]{1,0:T(8,128)(2,1)}, u32[]{:S(2)}, u32[]{:S(2)}) %collective-permute-start.3) | collective-permute-done | bytes 1048608 | tf_op jit(solution)/shard_map/ppermute | solution.py:25
  168.8 6.1 %collective-permute-done.2 = bf16[256,2048]{1,0:T(8,128)(2,1)} collective-permute-done((bf16[256,2048]{1,0:T(8,128)(2,1)}, bf16[256,2048]{1,0:T(8,128)(2,1)}, u32[]{:S(2)}, u32[]{:S(2)}) %collective-permute-start.2) | collective-permute-done | bytes 1048608 | tf_op jit(solution)/shard_map/ppermute | solution.py:22
  174.9 2.1 pad_maximum_fusion
  177.0 2.0 fusion.121
  179.0 2.6 copy.60
  181.6 2.6 copy.62
  184.2 11.4 %fusion.128 = (f32[16,256]{1,0:T(8,128)S(1)}, f32[16,256,768]{2,1,0:T(8,128)}) fusion(pred[256,768]{1,0:T(8,128)(4,1)S(1)} %fusion.90, bf16[256,16,64]{0,2,1:T(8,128)(2,1)} %bitcast.119, bf16[768,16,64]{0,2,1:T(8,128)(2,1)} %bitcast.115), kind=kOutput, calls=%fused_computation.199 | convolution fusion | flops 418382592 | bytes 14893056 | tf_op jit(solution)/shard_map/sub | solution.py:85
  195.6 7.1 %fusion.77 = bf16[16,64,256]{2,1,0:T(8,128)(2,1)S(1)} fusion(bf16[768,16,64]{0,2,1:T(8,128)(2,1)} %bitcast.114, f32[16,256,768]{2,1,0:T(8,128)} %get-tuple-element.54, f32[16,256]{1,0:T(8,128)S(1)} %get-tuple-element.53), kind=kOutput, calls=%fused_computation.103 | convolution fusion | flops 409206784 | bytes 14696448 | tf_op jit(solution)/shard_map/hqk,khd->qhd/dot_general | solution.py:87
  202.7 0.8 fusion.129
  203.6 1.0 copy-done.1
  204.6 0.2 multiply_reduce_fusion.1
  204.8 0.0 all-gather.13.cloned.1.call-done
  204.9 7.7 %copy.64 = bf16[2,4,8,16,4096]{4,3,2,1,0:T(8,128)(2,1)} copy(bf16[2,4,8,16,4096]{4,3,0,1,2:T(8,128)(2,1)} %bitcast.107) | data formatting | bytes 16777216 | tf_op jit(solution)/shard_map/transpose | solution.py:43
  212.6 74.4 %all-gather.9.cloned.1.call-done = bf16[64,16,4096]{2,1,0:T(8,128)(2,1)} async-done(((bf16[8,16,4096]{2,1,0:T(8,128)(2,1)}), bf16[64,16,4096]{2,1,0:T(8,128)(2,1)}) %all-gather.9.cloned.1.call-update) | async-done | bytes 8388624 | tf_op jit(solution)/shard_map/all_gather | solution.py:39
  287.0 7.8 %copy.63 = bf16[2,4,8,16,4096]{4,3,2,1,0:T(8,128)(2,1)} copy(bf16[2,4,8,16,4096]{4,3,0,1,2:T(8,128)(2,1)} %bitcast.108) | data formatting | bytes 16777216 | tf_op jit(solution)/shard_map/transpose | solution.py:43
  294.8 12.0 %fusion.130 = (f32[256]{0:T(256)S(1)}, f32[256,1024]{1,0:T(8,128)}) fusion(f32[256,1024]{1,0:T(8,128)S(1)} %copy-done.2, bf16[1024,4096]{1,0:T(8,128)(2,1)} %bitcast.109, bf16[1024,4096]{1,0:T(8,128)(2,1)} %bitcast.110, f32[1024]{0:T(1024)S(1)} %bitcast.129, f32[256]{0:T(256)S(1)} %add_rsqrt_fusion.1, f32[256]{0:T(256)S(1)} %broadcast_multiply_fusion.1), kind=kOutput, calls=%fused_computation.201 | convolution fusion | flops 4305977344 | bytes 18881536 | tf_op jit(solution)/shard_map/dot_general | solution.py:62
  306.8 1.5 multiply_reduce_fusion
  308.3 1.6 fusion.80
  309.9 5.4 %collective-permute-start.5 = (bf16[100,256]{1,0:T(8,128)(2,1)S(1)}, bf16[100,256]{1,0:T(8,128)(2,1)S(1)}, u32[]{:S(2)}, u32[]{:S(2)}) collective-permute-start(bf16[100,256]{1,0:T(8,128)(2,1)S(1)} %fusion.80), channel_id=1, source_target_pairs={{1,0},{2,1},{3,2},{4,3},{5,4},{6,5},{7,6},{8,7},{9,8},{10,9},{11,1... | collective-permute-start | bytes 153608 | tf_op jit(solution)/shard_map/ppermute | solution.py:25
  315.3 1.9 collective-permute-start.4
  317.3 0.9 slice.100
  318.2 0.9 copy.73
  319.1 6.5 %collective-permute-done.4 = bf16[100,256]{1,0:T(8,128)(2,1)S(1)} collective-permute-done((bf16[100,256]{1,0:T(8,128)(2,1)S(1)}, bf16[100,256]{1,0:T(8,128)(2,1)S(1)}, u32[]{:S(2)}, u32[]{:S(2)}) %collective-permute-start.4) | collective-permute-done | bytes 51232 | tf_op jit(solution)/shard_map/ppermute | solution.py:22
  325.6 0.2 copy.65
  325.8 2.8 gather_fusion.3
  328.6 2.8 gather_fusion.2
  331.4 4.0 %gather_fusion.1 = f32[1024,100]{1,0:T(8,128)} fusion(f32[100,768]{0,1:T(8,128)S(1)} %copy.65, s32[1024]{0:T(1024)S(1)} %fusion.110), kind=kCustom, calls=%fused_computation.1.clone | custom fusion | bytes 823296 | tf_op jit(solution)/shard_map/jit(_take)/gather | solution.py:154
  335.5 4.0 %gather_fusion = f32[1024,100]{1,0:T(8,128)} fusion(f32[100,768]{0,1:T(8,128)S(1)} %copy.65, s32[1024]{0:T(1024)S(1)} %fusion.109), kind=kCustom, calls=%fused_computation.clone | custom fusion | bytes 823296 | tf_op jit(solution)/shard_map/jit(_take)/gather | solution.py:154
  339.5 3.8 %fusion.93 = f32[100,1024]{0,1:T(8,128)} fusion(f32[1024,100]{1,0:T(8,128)S(1)} %gather_fusion.3, f32[1024,100]{1,0:T(8,128)S(1)} %gather_fusion.2, f32[1024,100]{1,0:T(8,128)} %gather_fusion.1, f32[1024,100]{1,0:T(8,128)} %gather_fusion, bf16[100,1024]{0,1:T(8,128)(2,1)} %copy.73, pred[1024]{0:T(1024)(128)(4,1)S(1)} %get-tuple-element.61, ...), kind=kLoop, calls=%fused_computation.121 | loop fusion | flops 1024000 | bytes 2256896 | tf_op jit(solution)/shard_map/add | solution.py:156
  343.3 3.7 all-to-all-start
  346.9 0.8 dynamic-slice_convert_fusion
  347.7 9.5 %all-to-all-done = f32[1,100,1024]{1,0,2:T(1,128)S(1)} async-done(((f32[1,100,1024]{1,0,2:T(1,128)}), f32[1,100,1024]{1,0,2:T(1,128)S(1)}, u32[]{:S(2)}, u32[]{:S(2)}) %all-to-all-start) | async-done | bytes 409632 | tf_op jit(solution)/shard_map/all_to_all | solution.py:159
  357.3 0.2 copy.70
  357.5 0.4 subtract_convert_fusion
  358.0 9.4 %all_to_all.27 = bf16[4,100,256]{2,1,0:T(8,128)(2,1)S(1)} all-to-all(bf16[4,100,256]{2,1,0:T(8,128)(2,1)S(1)} %subtract_convert_fusion), channel_id=1, replica_groups=mesh['member'=4,'node_0'=2,'node_1'=4,'node_2'=8] {'member'}, dimensions={0} | all-to-all | bytes 409600 | tf_op jit(solution)/shard_map/all_to_all | solution.py:169
  367.4 0.2 copy.71
  367.6 1.2 reshape.245
  (49 shorter events, 0.3 us)
Async XLA Ops:
  6.5 196.2 %copy-start = (bf16[1024,1024]{1,0:T(8,128)(2,1)S(1)}, bf16[1024,1024]{1,0:T(8,128)(2,1)}, u32[]{:S(2)}) copy-start(bf16[1024,1024]{1,0:T(8,128)(2,1)} %param.26) | copy-start | bytes 6291460
  6.5 65.8 %copy-start.4 = (bf16[218,1024]{1,0:T(8,128)(2,1)S(1)}, bf16[218,1024]{1,0:T(8,128)(2,1)}, u32[]{:S(2)}) copy-start(bf16[218,1024]{1,0:T(8,128)(2,1)} %param.16) | copy-start | bytes 1339396
  6.5 74.2 %copy-start.10 = (s32[256]{0:T(256)S(1)}, s32[256]{0:T(256)}, u32[]{:S(2)}) copy-start(s32[256]{0:T(256)} %param.19) | copy-start | bytes 3076
  6.5 74.2 %copy-start.5 = (s32[1024,4]{0,1:T(4,128)S(1)}, s32[1024,4]{0,1:T(4,128)}, u32[]{:S(2)}) copy-start(s32[1024,4]{0,1:T(4,128)} %param.21) | copy-start | bytes 49156
  6.5 74.3 %copy-start.6 = (s32[256,16]{0,1:T(8,128)S(1)}, s32[256,16]{0,1:T(8,128)}, u32[]{:S(2)}) copy-start(s32[256,16]{0,1:T(8,128)} %param.18) | copy-start | bytes 49156
  6.5 74.3 %copy-start.7 = (f32[3,1024]{1,0:T(4,128)S(1)}, f32[3,1024]{1,0:T(4,128)}, u32[]{:S(2)}) copy-start(f32[3,1024]{1,0:T(4,128)} %param.24) | copy-start | bytes 36868
  6.6 37.0 %all-gather.11.cloned.1.call-start = ((), (), s32[]{:S(2)}) async-start(), calls=%async_computation.4 | async-start | bytes 1310720 | tf_op jit(solution)/shard_map/all_gather | solution.py:39
  14.4 57.9 %all-gather.7.cloned.1.call-start = ((), (), s32[]{:S(2)}) async-start(), calls=%async_computation.2 | async-start | bytes 1310720 | tf_op jit(solution)/shard_map/all_gather | solution.py:39
  20.5 184.4 %all-gather.13.cloned.1.call-start = ((), (), s32[]{:S(2)}) async-start(), calls=%async_computation.5 | async-start | bytes 9437184 | tf_op jit(solution)/shard_map/all_gather | solution.py:39
  43.6 243.4 %all-gather.9.cloned.1.call-start = ((), (), s32[]{:S(2)}) async-start(), calls=%async_computation.3 | async-start | bytes 9437184 | tf_op jit(solution)/shard_map/all_gather | solution.py:39
  72.3 18.4 %collective-permute-start.1 = (bf16[218,1024]{1,0:T(8,128)(2,1)S(1)}, bf16[218,1024]{1,0:T(8,128)(2,1)S(1)}, u32[]{:S(2)}, u32[]{:S(2)}) collective-permute-start(bf16[218,1024]{1,0:T(8,128)(2,1)S(1)} %copy-done.4), channel_id=1, source_target_pairs={{1,0},{2,1},{3,2},{4,3},{5,4},{6,5},{7,6},{8,7},{9,8},{10,9},{11,1... | collective-permute-start | bytes 1339400 | tf_op jit(solution)/shard_map/ppermute | solution.py:25
  78.8 23.8 %collective-permute-start = (bf16[218,1024]{1,0:T(8,128)(2,1)S(1)}, bf16[218,1024]{1,0:T(8,128)(2,1)}, u32[]{:S(2)}, u32[]{:S(2)}) collective-permute-start(bf16[218,1024]{1,0:T(8,128)(2,1)S(1)} %copy-done.4), channel_id=1, source_target_pairs={{0,1},{1,2},{2,3},{3,4},{4,5},{5,6},{6,7},{7,8},{8,9},{9,10},{10,1... | collective-permute-start | bytes 1339400 | tf_op jit(solution)/shard_map/ppermute | solution.py:22
  90.7 11.8 %copy-start.12 = (bf16[218,1024]{1,0:T(8,128)(2,1)}, bf16[218,1024]{1,0:T(8,128)(2,1)S(1)}, u32[]{:S(2)}) copy-start(bf16[218,1024]{1,0:T(8,128)(2,1)S(1)} %collective-permute-done.1) | copy-start | bytes 1339396
  115.0 13.2 %copy-start.11 = (s32[256]{0:T(256)S(1)}, s32[256]{0:T(256)}, u32[]{:S(2)}) copy-start(s32[256]{0:T(256)} %param.20) | copy-start | bytes 3076
  121.1 47.7 %collective-permute-start.3 = (bf16[256,2048]{1,0:T(8,128)(2,1)}, bf16[256,2048]{1,0:T(8,128)(2,1)}, u32[]{:S(2)}, u32[]{:S(2)}) collective-permute-start(bf16[256,2048]{1,0:T(8,128)(2,1)} %slice.157), channel_id=1, source_target_pairs={{1,0},{2,1},{3,2},{4,3},{5,4},{6,5},{7,6},{8,7},{9,8},{10,9},{11,1... | collective-permute-start | bytes 3145736 | tf_op jit(solution)/shard_map/ppermute | solution.py:25
  123.0 52.0 %collective-permute-start.2 = (bf16[256,2048]{1,0:T(8,128)(2,1)}, bf16[256,2048]{1,0:T(8,128)(2,1)}, u32[]{:S(2)}, u32[]{:S(2)}) collective-permute-start(bf16[256,2048]{1,0:T(8,128)(2,1)} %slice.157), channel_id=1, source_target_pairs={{0,1},{1,2},{2,3},{3,4},{4,5},{5,6},{6,7},{7,8},{8,9},{9,10},{10,1... | collective-permute-start | bytes 3145736 | tf_op jit(solution)/shard_map/ppermute | solution.py:22
  203.5 1.0 copy-start.1
  287.0 7.8 %copy-start.2 = (f32[256,1024]{1,0:T(8,128)S(1)}, f32[256,1024]{1,0:T(8,128)}, u32[]{:S(2)}) copy-start(f32[256,1024]{1,0:T(8,128)} %copy-done.1) | copy-start | bytes 3145732
  294.8 13.5 %copy-start.3 = (bf16[1024,100]{0,1:T(8,128)(2,1)S(1)}, bf16[1024,100]{0,1:T(8,128)(2,1)}, u32[]{:S(2)}) copy-start(bf16[1024,100]{0,1:T(8,128)(2,1)} %param.29) | copy-start | bytes 614404
  309.9 9.2 %collective-permute-start.5 = (bf16[100,256]{1,0:T(8,128)(2,1)S(1)}, bf16[100,256]{1,0:T(8,128)(2,1)S(1)}, u32[]{:S(2)}, u32[]{:S(2)}) collective-permute-start(bf16[100,256]{1,0:T(8,128)(2,1)S(1)} %fusion.80), channel_id=1, source_target_pairs={{1,0},{2,1},{3,2},{4,3},{5,4},{6,5},{7,6},{8,7},{9,8},{10,9},{11,1... | collective-permute-start | bytes 153608 | tf_op jit(solution)/shard_map/ppermute | solution.py:25
  315.3 10.2 %collective-permute-start.4 = (bf16[100,256]{1,0:T(8,128)(2,1)S(1)}, bf16[100,256]{1,0:T(8,128)(2,1)S(1)}, u32[]{:S(2)}, u32[]{:S(2)}) collective-permute-start(bf16[100,256]{1,0:T(8,128)(2,1)S(1)} %fusion.80), channel_id=1, source_target_pairs={{0,1},{1,2},{2,3},{3,4},{4,5},{5,6},{6,7},{7,8},{8,9},{9,10},{10,1... | collective-permute-start | bytes 153608 | tf_op jit(solution)/shard_map/ppermute | solution.py:22
  331.4 8.1 %copy-start.8 = (pred[1024]{0:T(1024)(128)(4,1)S(1)}, pred[1024]{0:T(1024)(128)(4,1)}, u32[]{:S(2)}) copy-start(pred[1024]{0:T(1024)(128)(4,1)} %get-tuple-element.62) | copy-start | bytes 3076
  335.5 4.0 %copy-start.9 = (pred[1024]{0:T(1024)(128)(4,1)S(1)}, pred[1024]{0:T(1024)(128)(4,1)}, u32[]{:S(2)}) copy-start(pred[1024]{0:T(1024)(128)(4,1)} %get-tuple-element.63) | copy-start | bytes 3076
  343.3 14.0 %all-to-all-start = ((f32[1,100,1024]{1,0,2:T(1,128)}), f32[1,100,1024]{1,0,2:T(1,128)S(1)}, u32[]{:S(2)}, u32[]{:S(2)}) async-start(f32[1,100,1024]{1,0,2:T(1,128)} %bitcast.113), calls=%async_computation | async-start | bytes 1048576 | tf_op jit(solution)/shard_map/all_to_all | solution.py:159
Sparse Core Ops, SparseCore 0:
  14.5 29.0 all-gather.10
  45.4 26.8 all-gather.6
  74.1 120.2 all-gather.12
  196.0 90.8 all-gather.8
where the time goes:
time: 376 us; the launch traced here: 375 us
  waiting for transfers between devices  207 us (55%)
  matrix products  50.1 us (13%)
  local copies, waits for them, and re-layouts  45.2 us (12%)
  starting transfers between devices  25.3 us (7%)
  blocking collectives  23.1 us (6%)
  between operations  13.5 us (4%)
  other arithmetic  10.8 us (3%)
    all_gather x4, waiting for transfers between devices, gather_in_order(): blocks = lax.all_gather(blocks, axes[k], axis=0, tiled=True)  126 us
    ppermute x3, waiting for transfers between devices, with_halo(): lax.ppermute(lax.slice_in_dim(block, 0, width, axis=dim), axis, backward)  47.2 us
    ppermute x3, waiting for transfers between devices, with_halo(): lax.ppermute(lax.slice_in_dim(block, block.shape[dim] - width, None, axis...  24.5 us
    transpose x2, local copies, waits for them, and re-layouts, gather_in_order(): blocks.transpose(*turned, *range(len(sequence), blocks.ndim))  15.6 us
    all_gather x2, blocking collectives, gather_in_order(): blocks = lax.all_gather(blocks, axes[k], axis=0, tiled=True)  13.8 us
    ppermute x3, starting transfers between devices, with_halo(): lax.ppermute(lax.slice_in_dim(block, 0, width, axis=dim), axis, backward)  13.7 us
    gather x4, local copies, waits for them, and re-layouts, per_device(): summed = summed + jnp.take(projected_near, local_nodes[:, position], axis=1)  13.7 us
    dot_general x1, matrix products, per_device(): jnp.dot(pooled_nodes, embed_weight, preferred_element_type=jnp.float32)  12.2 us
  transfers between devices with their start and end apart: 11, of which 9 were waited for; matrix products, arithmetic and copies ran while one was open for 17% of the time, Pallas kernels for 0%

commit v1 on v0

v1 whole, which is shorter than its diff:
```python
import functools

import jax
import jax.numpy as jnp
from jax import lax
from jax.experimental import pallas as pl
from jax.experimental.pallas import tpu as pltpu
from jax.sharding import Mesh
from jax.sharding import PartitionSpec as P

HEADS = 16
HEAD_DIM = 64
BAND = 256
NODE = ("node_0", "node_1", "node_2")
MEMBER = ("member_hi", "member_core")

EPS = 1e-05
SMOOTH = 0.25

F32 = jnp.float32
BF16 = jnp.bfloat16
LANES_BOTH = (((1,), (1,)), ((), ()))


def params(mib):
    return pltpu.CompilerParams(vmem_limit_bytes=mib * 1024 * 1024)


def cost(flops, moved, transcendentals=0):
    return pl.CostEstimate(
        flops=int(flops), bytes_accessed=int(moved), transcendentals=int(transcendentals)
    )


def layer_norm(entries, scale_gain):
    average = jnp.mean(entries, axis=-1, keepdims=True)
    centred = entries - average
    variance = jnp.mean(centred * centred, axis=-1, keepdims=True)
    return centred * lax.rsqrt(variance + EPS) * scale_gain


def score_gradient(difference):
    return difference * lax.rsqrt(difference * difference + SMOOTH * SMOOTH)


def dot(left_side, right_side):
    return jnp.dot(left_side, right_side, preferred_element_type=F32)


def dot_lanes(left_side, right_side):
    return lax.dot_general(left_side, right_side, LANES_BOTH, preferred_element_type=F32)


def neighbours(block):
    count = lax.axis_size(NODE)
    forward = [(i, i + 1) for i in range(count - 1)]
    backward = [(target, source) for source, target in forward]
    return lax.ppermute(block, NODE, forward), lax.ppermute(block, NODE, backward)


def other_core(block):
    return lax.ppermute(block, "member_core", [(0, 1), (1, 0)])


def tally_kernel(slots_ref, out_ref):
    rows = 16
    width = out_ref.shape[1]
    chunk = 1024

    def body(step, carry):
        first = pl.multiple_of(step * rows, rows)
        slots = slots_ref[pl.ds(first, rows), :]
        for start in range(0, width, chunk):
            window = lax.broadcasted_iota(jnp.int32, (rows, chunk), 1) + start
            total = jnp.zeros((rows, chunk), F32)
            for position in range(slots.shape[1]):
                hit = slots[:, position : position + 1] == window
                total = total + jnp.where(hit, 1.0, 0.0)
            out_ref[pl.ds(first, rows), start : start + chunk] = total.astype(BF16)
        return carry

    lax.fori_loop(0, out_ref.shape[0] // rows, body, 0)


def encoder_tallies(slots, width):
    nodes, count = slots.shape
    return pl.pallas_call(
        tally_kernel,
        out_shape=jax.ShapeDtypeStruct((nodes, width), BF16),
        compiler_params=params(16),
        cost_estimate=cost(3 * nodes * width * count, nodes * width * 2),
        name="encoder_tallies",
    )(slots)


def pooled_kernel(tally_ref, low_ref, own_ref, high_ref, count_ref, out_ref):
    width = low_ref.shape[1]
    total = dot_lanes(tally_ref[:, width : 2 * width], own_ref[...])
    total = total + dot_lanes(tally_ref[:, :width], low_ref[...])
    total = total + dot_lanes(tally_ref[:, 2 * width :], high_ref[...])
    out_ref[...] = (total / count_ref[...]).astype(BF16)


def pool(tallies, low, own, high, counts):
    nodes = tallies.shape[0]
    channels = own.shape[0]
    return pl.pallas_call(
        pooled_kernel,
        out_shape=jax.ShapeDtypeStruct((nodes, channels), BF16),
        compiler_params=params(24),
        cost_estimate=cost(2 * nodes * tallies.shape[1] * channels, tallies.size * 4),
        name="pooled",
    )(tallies, low, own, high, counts)


def qkv_kernel(
    pool_low, pool_own, pool_high, per_low, per_own, per_high, embed_ref, gain_ref, qkv_hbm,
    start_ref, query_ref, kv_ref, qkv_ref, sem,
):
    copy = pltpu.make_async_copy(qkv_hbm, qkv_ref, sem)
    copy.start()
    nodes, width = start_ref.shape
    gain = gain_ref[0:1, :]

    def start_of(pooled, perturb):
        return dot(pooled[...], embed_ref[...]) + perturb[...].astype(F32)

    normed = []
    for place, (pooled, perturb) in enumerate(
        ((pool_low, per_low), (pool_own, per_own), (pool_high, per_high))
    ):
        start = start_of(pooled, perturb)
        if place == 1:
            start_ref[...] = start
        normed.append(layer_norm(start, gain).astype(BF16))
    copy.wait()
    query = dot(normed[1], qkv_ref[:, :width]).astype(BF16)
    query_ref[...] = query * jnp.asarray(HEAD_DIM ** (-0.5), BF16)
    for place in range(3):
        for half in range(2):
            columns = slice((half + 1) * width, (half + 2) * width)
            kv_ref[place * nodes : (place + 1) * nodes, half * width : (half + 1) * width] = dot(
                normed[place], qkv_ref[:, columns]
            ).astype(BF16)


def qkv(pooled, perturbs, embed_weight, norm_gains, qkv_weight):
    nodes, width = perturbs[1].shape
    vmem = pl.BlockSpec(memory_space=pltpu.VMEM)
    return pl.pallas_call(
        qkv_kernel,
        out_shape=(
            jax.ShapeDtypeStruct((nodes, width), F32),
            jax.ShapeDtypeStruct((nodes, width), BF16),
            jax.ShapeDtypeStruct((3 * nodes, 2 * width), BF16),
        ),
        in_specs=[vmem] * 8 + [pl.BlockSpec(memory_space=pl.ANY)],
        scratch_shapes=[pltpu.VMEM(qkv_weight.shape, BF16), pltpu.SemaphoreType.DMA],
        compiler_params=params(44),
        cost_estimate=cost(2 * 7 * nodes * width * width, 16 << 20),
        name="embed_qkv",
    )(*pooled, *perturbs, embed_weight, norm_gains, qkv_weight)


def attention_kernel(
    where_ref, query_ref, kv_ref, reach_ref, start_ref, gain_ref, out_hbm,
    mid_ref, normed_ref, cap_ref, attended_ref, out_ref, sem,
):
    copy = pltpu.make_async_copy(out_hbm, out_ref, sem)
    copy.start()
    nodes, width = query_ref.shape
    rows = cap_ref.shape[1]
    span = cap_ref.shape[2]
    first_query = where_ref[0]
    node_total = where_ref[1]
    for block in range(nodes // rows):
        at = first_query + block * rows + lax.broadcasted_iota(jnp.int32, (rows, span), 0)
        key = first_query - BAND + block * rows + lax.broadcasted_iota(jnp.int32, (rows, span), 1)
        reach = reach_ref[block * rows : (block + 1) * rows, :]
        allowed = (jnp.abs(at - key) <= reach) & (key >= 0) & (key < node_total)
        cap_ref[block] = jnp.where(allowed, 3e38, -1e30)

    lane = lax.broadcasted_iota(jnp.int32, (1, 2 * HEAD_DIM), 1)
    for block in range(nodes // rows):
        cap = cap_ref.at[block]
        for pair in range(HEADS // 2):
            columns = slice(pair * 2 * HEAD_DIM, (pair + 1) * 2 * HEAD_DIM)
            value_columns = slice(width + pair * 2 * HEAD_DIM, width + (pair + 1) * 2 * HEAD_DIM)
            queries = query_ref[block * rows : (block + 1) * rows, columns]
            keys = kv_ref[block * rows : block * rows + span, columns]
            values = kv_ref[block * rows : block * rows + span, value_columns]
            halves = []
            for side in range(2):
                mine = (lane < HEAD_DIM) if side == 0 else (lane >= HEAD_DIM)
                chosen = jnp.where(mine, queries, jnp.zeros_like(queries))
                scores = jnp.minimum(dot_lanes(chosen, keys), cap[...])
                highest = jnp.max(scores, axis=-1, keepdims=True)
                weights = jnp.exp(scores - highest)
                total = jnp.sum(weights, axis=-1, keepdims=True)
                blended = dot(weights.astype(BF16), values)
                halves.append(blended * (1.0 / total))
            attended_ref[block * rows : (block + 1) * rows, columns] = jnp.where(
                lane < HEAD_DIM, halves[0], halves[1]
            ).astype(BF16)
    copy.wait()
    middle = start_ref[...] + dot(attended_ref[...], out_ref[...])
    mid_ref[...] = middle
    normed_ref[...] = layer_norm(middle, gain_ref[1:2, :]).astype(BF16)


def attention(where, query, kv, reach, start, norm_gains, out_weight):
    nodes, width = query.shape
    rows = 128
    span = rows + 2 * BAND
    vmem = pl.BlockSpec(memory_space=pltpu.VMEM)
    return pl.pallas_call(
        attention_kernel,
        out_shape=(
            jax.ShapeDtypeStruct((nodes, width), F32),
            jax.ShapeDtypeStruct((nodes, width), BF16),
        ),
        in_specs=[pl.BlockSpec(memory_space=pltpu.SMEM)]
        + [vmem] * 5
        + [pl.BlockSpec(memory_space=pl.ANY)],
        scratch_shapes=[
            pltpu.VMEM((nodes // rows, rows, span), F32),
            pltpu.VMEM((nodes, width), BF16),
            pltpu.VMEM(out_weight.shape, BF16),
            pltpu.SemaphoreType.DMA,
        ],
        compiler_params=params(32),
        cost_estimate=cost(
            4 * nodes * span * width + 2 * nodes * width * width,
            10 << 20,
            nodes * span * HEADS,
        ),
        name="attention",
    )(where, query, kv, reach, start, norm_gains, out_weight)


def mlp_kernel(tokens_ref, weight_ref, out_ref):
    blocks, sides, rows, columns = weight_ref.shape
    rows = rows // 2
    part = blocks * rows

    upper = None
    for side in range(sides):
        up = weight_ref[:, side, :rows, :].reshape(part, columns)
        term = dot(tokens_ref[:, side * part : (side + 1) * part], up)
        upper = term if upper is None else upper + term
    active = jax.nn.gelu(upper).astype(BF16)
    lowered = []
    for side in range(sides):
        down = weight_ref[:, side, rows:, :].reshape(part, columns)
        lowered.append(dot_lanes(active, down))

    @pl.when(pl.program_id(0) == 0)
    def _():
        for side in range(sides):
            out_ref[:, side * part : (side + 1) * part] = lowered[side]

    @pl.when(pl.program_id(0) > 0)
    def _():
        for side in range(sides):
            out_ref[:, side * part : (side + 1) * part] += lowered[side]


def mlp_part(tokens, weights):
    nodes, width = tokens.shape
    blocks, sides, rows, hidden = weights.shape
    step = 512
    return pl.pallas_call(
        mlp_kernel,
        grid=(hidden // step,),
        out_shape=jax.ShapeDtypeStruct((nodes, width), F32),
        in_specs=[
            pl.BlockSpec((nodes, width), lambda j: (0, 0)),
            pl.BlockSpec((blocks, sides, rows, step), lambda j: (0, 0, 0, j)),
        ],
        out_specs=pl.BlockSpec((nodes, width), lambda j: (0, 0)),
        compiler_params=params(32),
        cost_estimate=cost(4 * nodes * width * hidden, weights.size * 2, nodes * hidden),
        name="mlp_part",
    )(tokens, weights)


def head_kernel(mid_ref, own_ref, other_ref, gain_ref, head_ref, out_ref):
    ending = mid_ref[...] + (own_ref[...] + other_ref[...])
    final = layer_norm(ending, gain_ref[2:3, :]).astype(BF16)
    out_ref[...] = dot_lanes(head_ref[...], final).astype(BF16)


def head(middle, own, other, norm_gains, head_rows):
    nodes, width = middle.shape
    variables = head_rows.shape[0]
    return pl.pallas_call(
        head_kernel,
        out_shape=jax.ShapeDtypeStruct((variables, nodes), BF16),
        compiler_params=params(24),
        cost_estimate=cost(2 * nodes * width * variables, 4 << 20),
        name="final_head",
    )(middle, own, other, norm_gains, head_rows)


def decoder_tally_kernel(slots_ref, out_ref):
    rows = 64
    points = out_ref.shape[1]
    slots = slots_ref.shape[0]

    def body(step, carry):
        first = pl.multiple_of(step * rows, rows)
        node = first + lax.broadcasted_iota(jnp.int32, (rows, points), 0)
        total = jnp.zeros((rows, points), F32)
        for position in range(slots):
            hit = slots_ref[position : position + 1, :] == node
            total = total + jnp.where(hit, 1.0 / slots, 0.0)
        out_ref[pl.ds(first, rows), :] = total.astype(BF16)
        return carry

    lax.fori_loop(0, out_ref.shape[0] // rows, body, 0)


def decoder_tallies(slots, nodes):
    count, points = slots.shape
    return pl.pallas_call(
        decoder_tally_kernel,
        out_shape=jax.ShapeDtypeStruct((nodes, points), BF16),
        compiler_params=params(16),
        cost_estimate=cost(3 * nodes * points * count, nodes * points * 2),
        name="decoder_tallies",
    )(slots)


def crps_kernel(tally_ref, state_ref, truth_ref, *refs):
    out_ref = refs[-1]
    refs = refs[:-1]
    variables = out_ref.shape[0]
    nodes = refs[0].shape[1]
    state = state_ref[:variables, :].astype(F32)
    forecasts = []
    for member in range(len(refs) // 3):
        field = None
        for place in range(3):
            term = dot(
                refs[3 * member + place][...], tally_ref[place * nodes : (place + 1) * nodes, :]
            )
            field = term if field is None else field + term
        forecasts.append(state + field)
    members = len(forecasts)
    own = forecasts[0]
    pairwise = None
    for other in forecasts:
        term = score_gradient(own - other)
        pairwise = term if pairwise is None else pairwise + term
    out_ref[...] = score_gradient(own - truth_ref[...].astype(F32)) * (
        1.0 / members
    ) - pairwise * (1.0 / (members * (members - 1)))


def crps(tallies, state, truth, projected):
    variables, points = truth.shape
    return pl.pallas_call(
        crps_kernel,
        out_shape=jax.ShapeDtypeStruct((variables, points), F32),
        compiler_params=params(32),
        cost_estimate=cost(2 * 4 * variables * points * tallies.shape[0], 4 << 20),
        name="decoder_crps",
    )(tallies, state, truth, *projected)


def per_device(
    gridpoint_state,
    grid_truth,
    encoder_slots,
    encoder_count,
    node_reach,
    decoder_slots,
    member_perturb,
    embed_weight,
    norm_gains,
    qkv_weight,
    out_weight,
    up_weight,
    down_weight,
    head_weight,
):
    region = lax.axis_index(NODE)
    region_count = lax.axis_size(NODE)
    core = lax.axis_index("member_core")
    grid_dev = gridpoint_state.shape[1]
    node_dev = encoder_slots.shape[0]
    hidden = up_weight.shape[1] // 2
    perturb = member_perturb[0]

    share = jnp.concatenate(
        [
            lax.dynamic_slice_in_dim(up_weight, core * hidden, hidden, 1),
            lax.dynamic_slice_in_dim(down_weight, core * hidden, hidden, 1),
        ],
        axis=0,
    )
    pair = lax.all_gather(share, NODE[0], axis=0)
    weights = lax.all_gather(pair, NODE[1:], axis=0)

    state_low, state_high = neighbours(gridpoint_state)
    perturb_low, perturb_high = neighbours(perturb)

    positions = jnp.arange(encoder_slots.shape[1], dtype=jnp.int32)
    local_slots = jnp.where(
        positions[None, :] < encoder_count[:, None],
        encoder_slots - (region - 1) * grid_dev,
        -1,
    )
    tallies = encoder_tallies(local_slots, 3 * grid_dev)
    near_slots = (decoder_slots - (region - 1) * node_dev).T
    decoder_near = decoder_tallies(near_slots, 3 * node_dev)
    counts = encoder_count[:, None].astype(F32)
    pooled = pool(tallies, state_low, gridpoint_state, state_high, counts)
    pooled_low, pooled_high = neighbours(pooled)
    start, query, kv = qkv(
        (pooled_low, pooled, pooled_high),
        (perturb_low, perturb, perturb_high),
        embed_weight,
        norm_gains,
        qkv_weight,
    )
    where = jnp.stack([region * node_dev, jnp.int32(region_count * node_dev)])
    middle, normed_mid = attention(
        where, query, kv, node_reach[:, None], start, norm_gains, out_weight
    )

    normed_other = other_core(normed_mid)
    part_other = mlp_part(normed_other, weights)
    part_mine = mlp_part(normed_mid, weights)
    projected = head(middle, part_mine, other_core(part_other), norm_gains, head_weight.T)

    both = jnp.stack([projected, other_core(projected)])
    axes = ("member_hi",) + NODE
    def sent(step, flip):
        links = []
        for side in range(2):
            for i in range(region_count):
                j = i + step
                if 0 <= j < region_count:
                    target = (1 - side) if flip else side
                    links.append((side * region_count + i, target * region_count + j))
        return lax.ppermute(both, axes, links)

    low, high = sent(1, False), sent(-1, False)
    far_low, far_own, far_high = sent(1, True), sent(0, True), sent(-1, True)
    projected_all = []
    for near in ((low, both, high), (far_low, far_own, far_high)):
        for k in range(2):
            projected_all += [block[k] for block in near]
    gradient = crps(decoder_near, gridpoint_state, grid_truth, projected_all)
    return gradient[None]


def solution(mesh):
    torus = Mesh(
        mesh.devices.reshape(2, 2, 2, 4, 8),
        MEMBER + NODE,
    )
    return jax.shard_map(
        per_device,
        mesh=torus,
        in_specs=(
            P(None, NODE),
            P(None, NODE),
            P(NODE, None),
            P(NODE),
            P(NODE),
            P(NODE, None),
            P(MEMBER, NODE, None),
            P(),
            P(),
            P(),
            P(),
            P(NODE, None),
            P(NODE, None),
            P(),
        ),
        out_specs=P(MEMBER, None, NODE),
        check_vma=False,
    )
```

time: 376 us -> 171 us (0.45)
  waiting for transfers between devices: 207 us -> 51 us
  matrix products: 50.1 us -> 0 us
  Pallas kernels: 0 us -> 39.1 us
  local copies, waits for them, and re-layouts: 45.2 us -> 6.63 us
  starting transfers between devices: 25.3 us -> 51.9 us
  blocking collectives: 23.1 us -> 6.15 us
  other arithmetic: 10.8 us -> 2.29 us
    all_gather x4 -> x1, waiting for transfers between devices: 126 us -> 36.7 us  [per_device(): weights = lax.all_gather(pair, NODE[1:], axis=0)]
    ppermute x6 -> x14, waiting for transfers between devices: 71.7 us -> 14.3 us  [the longest x5 8.8 us: sent(): return lax.ppermute(both, axes, links)]
    pallas_call x0 -> x9, Pallas kernels: none -> 39.1 us  [the longest x1 11.9 us: attention(): pl.pallas_call(attention_kernel, out_shape=(jax.ShapeDtypeStruct((nodes,...]
    dot_general x6 -> x0, matrix products: 38.7 us -> none  [the longest x1 12.2 us: per_device(): jnp.dot(pooled_nodes, embed_weight, preferred_element_type=jnp.float32)]
    ppermute x6 -> x14, starting transfers between devices: 21.5 us -> 51.9 us  [the longest x3 24.2 us: neighbours(): lax.ppermute(block, NODE, backward)]
    transpose x2 -> x0, local copies, waits for them, and re-layouts: 15.6 us -> none  [gather_in_order(): blocks.transpose(*turned, *range(len(sequence), blocks.ndim))]
    gather x4 -> x0, local copies, waits for them, and re-layouts: 13.7 us -> none  [per_device(): summed = summed + jnp.take(projected_near, local_nodes[:, position], axis=1)]
    slice x10 -> x0, local copies, waits for them, and re-layouts: 12.2 us -> none  [the longest x2 4.58 us: banded_attention(): key_heads = bordered[:, :model_width].reshape(key_count, HEADS, HEAD_DIM)]
  transfers between devices with their start and end apart: 11 -> 15, of which waited for: 9 -> 7; matrix products, arithmetic and copies ran while one was open for 17% -> 2% of each run, Pallas kernels for 0% -> 19%
where the time goes in v1:
time: 171 us
  starting transfers between devices  51.9 us (30%)
  waiting for transfers between devices  51 us (30%)
  Pallas kernels  39.1 us (23%)
  between operations  13.8 us (8%)
  local copies, waits for them, and re-layouts  6.63 us (4%)
  blocking collectives  6.15 us (4%)
  other arithmetic  2.29 us (1%)
    all_gather x1, waiting for transfers between devices, per_device(): weights = lax.all_gather(pair, NODE[1:], axis=0)  36.7 us
    ppermute x3, starting transfers between devices, neighbours(): lax.ppermute(block, NODE, backward)  24.2 us
    ppermute x5, starting transfers between devices, sent(): return lax.ppermute(both, axes, links)  19.2 us
    pallas_call x1, Pallas kernels, attention(): pl.pallas_call(attention_kernel, out_shape=(jax.ShapeDtypeStruct((nodes,...  11.9 us
    pallas_call x2, Pallas kernels, mlp_part(): pl.pallas_call(mlp_kernel, grid=(hidden // step,), out_shape=jax.ShapeDty...  9.03 us
    ppermute x5, waiting for transfers between devices, sent(): return lax.ppermute(both, axes, links)  8.8 us
    pallas_call x1, Pallas kernels, qkv(): pl.pallas_call(qkv_kernel, out_shape=(jax.ShapeDtypeStruct((nodes, width)...  7.96 us
    ppermute x3, starting transfers between devices, neighbours(): lax.ppermute(block, NODE, forward)  7.67 us
  transfers between devices with their start and end apart: 15, of which 7 were waited for; matrix products, arithmetic and copies ran while one was open for 2% of the time, Pallas kernels for 19%

profile of v1, /device:TPU:8, one launch (start us, length us, event | category | flops | bytes accessed | tf_op | source)
XLA Modules:
  0.0 170.9 jit_solution(15770025241174352703)
XLA Ops:
  6.5 0.0 all-gather.4.cloned.1.call-start
  6.5 0.9 constant_dynamic-slice_fusion
  7.5 0.0 copy-start.6
  7.5 0.0 copy-start.7
  7.5 0.0 copy-start.8
  7.5 6.2 %all-gather = bf16[64,2048]{1,0:T(8,128)(2,1)} all-gather(bf16[32,2048]{1,0:T(8,128)(2,1)S(1)} %pad_maximum_fusion), channel_id=2, replica_groups=mesh['member_hi'=2,'member_core'=2,'node_0'=2,'node_1'=4,'node_2'=8] {'n..., dimensions={0}, use_global_device_ids=true | all-gather | bytes 393216 | tf_op jit(solution)/shard_map/all_gather | solution.py:402
  13.7 0.0 all-gather.4.cloned.1.call-update
  13.7 3.8 %collective-permute-start = (bf16[218,1024]{1,0:T(8,128)(2,1)}, bf16[218,1024]{1,0:T(8,128)(2,1)S(1)}, u32[]{:S(2)}, u32[]{:S(2)}) collective-permute-start(bf16[218,1024]{1,0:T(8,128)(2,1)} %state_ref.1), channel_id=1, source_target_pairs={{0,1},{1,2},{2,3},{3,4},{4,5},{5,6},{6,7},{7,8},{8,9},{9,10},{10,1... | collective-permute-start | bytes 1339400 | tf_op jit(solution)/shard_map/ppermute | solution.py:58
  17.5 7.9 %collective-permute-start.1 = (bf16[218,1024]{1,0:T(8,128)(2,1)}, bf16[218,1024]{1,0:T(8,128)(2,1)S(1)}, u32[]{:S(2)}, u32[]{:S(2)}) collective-permute-start(bf16[218,1024]{1,0:T(8,128)(2,1)} %state_ref.1), channel_id=1, source_target_pairs={{1,0},{2,1},{3,2},{4,3},{5,4},{6,5},{7,6},{8,7},{9,8},{10,9},{11,1... | collective-permute-start | bytes 1339400 | tf_op jit(solution)/shard_map/ppermute | solution.py:58
  25.5 1.9 %collective-permute-start.4 = (bf16[256,1024]{1,0:T(8,128)(2,1)}, bf16[256,1024]{1,0:T(8,128)(2,1)}, u32[]{:S(2)}, u32[]{:S(2)}) collective-permute-start(bf16[256,1024]{1,0:T(8,128)(2,1)} %bitcast.38), channel_id=1, source_target_pairs={{0,1},{1,2},{2,3},{3,4},{4,5},{5,6},{6,7},{7,8},{8,9},{9,10},{10,1... | collective-permute-start | bytes 1572872 | tf_op jit(solution)/shard_map/ppermute | solution.py:58
  27.4 8.1 %collective-permute-start.5 = (bf16[256,1024]{1,0:T(8,128)(2,1)}, bf16[256,1024]{1,0:T(8,128)(2,1)}, u32[]{:S(2)}, u32[]{:S(2)}) collective-permute-start(bf16[256,1024]{1,0:T(8,128)(2,1)} %bitcast.39), channel_id=1, source_target_pairs={{1,0},{2,1},{3,2},{4,3},{5,4},{6,5},{7,6},{8,7},{9,8},{10,9},{11,1... | collective-permute-start | bytes 1572872 | tf_op jit(solution)/shard_map/ppermute | solution.py:58
  35.6 0.7 broadcast_subtract_fusion
  36.3 0.1 copy.28
  36.4 0.7 convert_element_type.5
  37.1 0.1 copy.29.count_ref
  37.2 0.8 copy.30.reach_ref
  38.1 0.8 fusion.slots_ref
  38.8 6.5 %encoder_tallies.1.tally_ref = bf16[256,3072]{1,0:T(8,128)(2,1)S(1)} custom-call(s32[256,16]{1,0:T(8,128)S(1)} %fusion.slots_ref), custom_call_target="tpu_custom_call" | custom-call | flops 37748736 | bytes 1572864 | tf_op jit(solution)/shard_map/encoder_tallies/pallas_call | solution.py:87
  45.4 0.0 collective-permute-done.low_ref
  45.4 0.0 collective-permute-done.1.high_ref
  45.4 0.0 copy-done.3
  45.4 0.6 pooled.1.pool_own
  46.0 1.9 %collective-permute-start.2 = (bf16[256,218]{1,0:T(8,128)(2,1)S(1)}, bf16[256,218]{1,0:T(8,128)(2,1)S(1)}, u32[]{:S(2)}, u32[]{:S(2)}) collective-permute-start(bf16[256,218]{1,0:T(8,128)(2,1)S(1)} %pooled.1.pool_own), channel_id=1, source_target_pairs={{0,1},{1,2},{2,3},{3,4},{4,5},{5,6},{6,7},{7,8},{8,9},{9,10},{10,1... | collective-permute-start | bytes 334856 | tf_op jit(solution)/shard_map/ppermute | solution.py:58
  47.9 8.1 %collective-permute-start.3 = (bf16[256,218]{1,0:T(8,128)(2,1)S(1)}, bf16[256,218]{1,0:T(8,128)(2,1)S(1)}, u32[]{:S(2)}, u32[]{:S(2)}) collective-permute-start(bf16[256,218]{1,0:T(8,128)(2,1)S(1)} %pooled.1.pool_own), channel_id=1, source_target_pairs={{1,0},{2,1},{3,2},{4,3},{5,4},{6,5},{7,6},{8,7},{9,8},{10,9},{11,1... | collective-permute-start | bytes 334856 | tf_op jit(solution)/shard_map/ppermute | solution.py:58
  56.1 0.1 pad_add_fusion.where_ref
  56.1 0.0 collective-permute-done.4.per_low
  56.2 0.0 collective-permute-done.5.per_high
  56.2 1.5 collective-permute-done.2.pool_low
  57.7 1.2 collective-permute-done.3.pool_high
  58.9 0.0 copy-done.6
  58.9 0.0 copy-done.7
  58.9 0.0 copy-done.8
  58.9 8.0 %embed_qkv.1 = (f32[256,1024]{1,0:T(8,128)S(1)}, bf16[256,1024]{1,0:T(8,128)(2,1)S(1)}, bf16[768,2048]{1,0:T(8,128)(2,1)S(1)}) custom-call(bf16[256,218]{1,0:T(8,128)(2,1)S(1)} %collective-permute-done.2.pool_low, bf16[256,218]{1,0:T(8,128)(2,1)S(1)} %pooled.1.pool_own, bf16[256,218]{1,0:T(8,128)(2,1)S(1)} %collective-permute-done.3.pool_high, ...), custom_call_target="tpu_custom_call" | custom-call | flops 3758096384 | bytes 16777216 | tf_op jit(solution)/shard_map/embed_qkv/pallas_call | solution.py:150
  66.9 11.9 %attention.1 = (f32[256,1024]{1,0:T(8,128)S(1)}, bf16[256,1024]{1,0:T(8,128)(2,1)S(1)}) custom-call(s32[2]{0:T(128)S(1)} %pad_add_fusion.where_ref, bf16[256,1024]{1,0:T(8,128)(2,1)S(1)} %get-tuple-element.10.query_ref, bf16[768,2048]{1,0:T(8,128)(2,1)S(1)} %get-tuple-element.11.kv_ref, s32[256,1]{1,0:T(8,128)S(1)} %copy.30.reach_ref, ...), custom_call_target="tpu_custom_call" | custom-call | flops 1207959552 | bytes 10485760 | tf_op jit(solution)/shard_map/attention/pallas_call | solution.py:216
  78.7 0.1 collective-permute-start.6
  78.8 1.9 %collective-permute-done.6.tokens_ref = bf16[256,1024]{1,0:T(8,128)(2,1)S(1)} collective-permute-done((bf16[256,1024]{1,0:T(8,128)(2,1)S(1)}, bf16[256,1024]{1,0:T(8,128)(2,1)S(1)}, u32[]{:S(2)}, u32[]{:S(2)}) %collective-permute-start.6) | collective-permute-done | bytes 524320 | tf_op jit(solution)/shard_map/ppermute | solution.py:62
  80.7 36.7 %all-gather.4.cloned.1.call-done = bf16[64,32,2048]{2,1,0:T(8,128)(2,1)} async-done(((bf16[2,32,2048]{2,1,0:T(8,128)(2,1)}), bf16[64,32,2048]{2,1,0:T(8,128)(2,1)}) %all-gather.4.cloned.1.call-update) | async-done | bytes 8388624 | tf_op jit(solution)/shard_map/all_gather | solution.py:403
  117.4 3.4 %copy-done = bf16[64,32,2048]{2,1,0:T(8,128)(2,1)S(1)} copy-done((bf16[64,32,2048]{2,1,0:T(8,128)(2,1)S(1)}, bf16[64,32,2048]{2,1,0:T(8,128)(2,1)}, u32[]{:S(2)}) %copy-start) | copy-done | bytes 8388632
  120.8 4.5 %mlp_part.3 = f32[256,1024]{1,0:T(8,128)S(1)} custom-call(bf16[256,1024]{1,0:T(8,128)(2,1)S(1)} %collective-permute-done.6.tokens_ref, bf16[32,2,32,2048]{3,2,1,0:T(8,128)(2,1)S(1)} %bitcast.32), custom_call_target="tpu_custom_call" | custom-call | flops 2147483648 | bytes 8388608 | tf_op jit(solution)/shard_map/mlp_part/pallas_call | solution.py:272
  125.3 0.0 copy-start.5
  125.3 0.1 collective-permute-start.7
  125.4 0.0 copy-done.1
  125.4 4.5 %mlp_part.2.own_ref = f32[256,1024]{1,0:T(8,128)S(1)} custom-call(bf16[256,1024]{1,0:T(8,128)(2,1)S(1)} %get-tuple-element.14.tokens_ref, bf16[32,2,32,2048]{3,2,1,0:T(8,128)(2,1)S(1)} %bitcast.33), custom_call_target="tpu_custom_call" | custom-call | flops 2147483648 | bytes 8388608 | tf_op jit(solution)/shard_map/mlp_part/pallas_call | solution.py:272
  129.9 0.0 copy-start.9
  130.0 0.0 collective-permute-done.7.other_ref
  130.0 0.0 copy-done.5
  130.0 0.0 copy-start.4
  130.0 0.6 final_head.1.refs_1_
  130.6 0.6 collective-permute-start.8
  131.2 0.9 collective-permute-done.8.refs_4_
  132.1 4.5 %collective-permute-start.13 = (bf16[2,100,256]{2,1,0:T(8,128)(2,1)S(1)}, bf16[2,100,256]{2,1,0:T(8,128)(2,1)S(1)}, u32[]{:S(2)}, u32[]{:S(2)}) collective-permute-start(bf16[2,100,256]{2,1,0:T(8,128)(2,1)S(1)} %pad_maximum_fusion.1), channel_id=1, source_target_pairs={{1,128},{2,129},{3,130},{4,131},{5,132},{6,133},{7,134},{8,135},{9... | collective-permute-start | bytes 307208 | tf_op jit(solution)/shard_map/ppermute | solution.py:447
  136.6 0.0 copy-done.9
  136.6 1.2 decoder_tallies.1.tally_ref
  137.9 1.2 collective-permute-start.12
  139.1 4.7 %collective-permute-start.11 = (bf16[2,100,256]{2,1,0:T(8,128)(2,1)S(1)}, bf16[2,100,256]{2,1,0:T(8,128)(2,1)S(1)}, u32[]{:S(2)}, u32[]{:S(2)}) collective-permute-start(bf16[2,100,256]{2,1,0:T(8,128)(2,1)S(1)} %pad_maximum_fusion.1), channel_id=1, source_target_pairs={{0,129},{1,130},{2,131},{3,132},{4,133},{5,134},{6,135},{7,136},{8... | collective-permute-start | bytes 307208 | tf_op jit(solution)/shard_map/ppermute | solution.py:447
  143.8 6.9 %collective-permute-start.10 = (bf16[2,100,256]{2,1,0:T(8,128)(2,1)S(1)}, bf16[2,100,256]{2,1,0:T(8,128)(2,1)S(1)}, u32[]{:S(2)}, u32[]{:S(2)}) collective-permute-start(bf16[2,100,256]{2,1,0:T(8,128)(2,1)S(1)} %pad_maximum_fusion.1), channel_id=1, source_target_pairs={{1,0},{2,1},{3,2},{4,3},{5,4},{6,5},{7,6},{8,7},{9,8},{10,9},{11,1... | collective-permute-start | bytes 307208 | tf_op jit(solution)/shard_map/ppermute | solution.py:447
  150.7 1.9 %collective-permute-start.9 = (bf16[2,100,256]{2,1,0:T(8,128)(2,1)S(1)}, bf16[2,100,256]{2,1,0:T(8,128)(2,1)S(1)}, u32[]{:S(2)}, u32[]{:S(2)}) collective-permute-start(bf16[2,100,256]{2,1,0:T(8,128)(2,1)S(1)} %pad_maximum_fusion.1), channel_id=1, source_target_pairs={{0,1},{1,2},{2,3},{3,4},{4,5},{5,6},{6,7},{7,8},{8,9},{9,10},{10,1... | collective-permute-start | bytes 307208 | tf_op jit(solution)/shard_map/ppermute | solution.py:447
  152.6 0.0 collective-permute-done.13
  152.6 0.0 collective-permute-done.12
  152.7 0.0 collective-permute-done.11
  152.7 0.3 collective-permute-done.10
  153.0 8.5 %collective-permute-done.9 = bf16[2,100,256]{2,1,0:T(8,128)(2,1)S(1)} collective-permute-done((bf16[2,100,256]{2,1,0:T(8,128)(2,1)S(1)}, bf16[2,100,256]{2,1,0:T(8,128)(2,1)S(1)}, u32[]{:S(2)}, u32[]{:S(2)}) %collective-permute-start.9) | collective-permute-done | bytes 102432 | tf_op jit(solution)/shard_map/ppermute | solution.py:447
  161.5 1.3 decoder_crps.1
  162.8 1.2 copy.31
  (14 shorter events, 0.1 us)
Async XLA Ops:
  6.5 38.8 %copy-start.3 = (bf16[218,1024]{1,0:T(8,128)(2,1)S(1)}, bf16[218,1024]{1,0:T(8,128)(2,1)}, u32[]{:S(2)}) copy-start(bf16[218,1024]{1,0:T(8,128)(2,1)} %state_ref.1) | copy-start | bytes 1339396
  6.5 110.9 %all-gather.4.cloned.1.call-start = ((), (), s32[]{:S(2)}) async-start(), calls=%async_computation | async-start | bytes 8650752 | tf_op jit(solution)/shard_map/all_gather | solution.py:403
  7.5 51.4 %copy-start.6 = (f32[3,1024]{1,0:T(4,128)S(1)}, f32[3,1024]{1,0:T(4,128)}, u32[]{:S(2)}) copy-start(f32[3,1024]{1,0:T(4,128)} %gain_ref.5) | copy-start | bytes 36868
  7.5 51.4 %copy-start.7 = (bf16[1,256,1024]{2,1,0:T(8,128)(2,1)S(1)}, bf16[1,256,1024]{2,1,0:T(8,128)(2,1)}, u32[]{:S(2)}) copy-start(bf16[1,256,1024]{2,1,0:T(8,128)(2,1)} %param.20) | copy-start | bytes 1572868
  7.5 51.4 %copy-start.8 = (bf16[218,1024]{1,0:T(8,128)(2,1)S(1)}, bf16[218,1024]{1,0:T(8,128)(2,1)}, u32[]{:S(2)}) copy-start(bf16[218,1024]{1,0:T(8,128)(2,1)} %embed_ref.1) | copy-start | bytes 1339396
  13.7 31.6 %collective-permute-start = (bf16[218,1024]{1,0:T(8,128)(2,1)}, bf16[218,1024]{1,0:T(8,128)(2,1)S(1)}, u32[]{:S(2)}, u32[]{:S(2)}) collective-permute-start(bf16[218,1024]{1,0:T(8,128)(2,1)} %state_ref.1), channel_id=1, source_target_pairs={{0,1},{1,2},{2,3},{3,4},{4,5},{5,6},{6,7},{7,8},{8,9},{9,10},{10,1... | collective-permute-start | bytes 1339400 | tf_op jit(solution)/shard_map/ppermute | solution.py:58
  17.5 27.8 %collective-permute-start.1 = (bf16[218,1024]{1,0:T(8,128)(2,1)}, bf16[218,1024]{1,0:T(8,128)(2,1)S(1)}, u32[]{:S(2)}, u32[]{:S(2)}) collective-permute-start(bf16[218,1024]{1,0:T(8,128)(2,1)} %state_ref.1), channel_id=1, source_target_pairs={{1,0},{2,1},{3,2},{4,3},{5,4},{6,5},{7,6},{8,7},{9,8},{10,9},{11,1... | collective-permute-start | bytes 1339400 | tf_op jit(solution)/shard_map/ppermute | solution.py:58
  25.5 30.7 %collective-permute-start.4 = (bf16[256,1024]{1,0:T(8,128)(2,1)}, bf16[256,1024]{1,0:T(8,128)(2,1)}, u32[]{:S(2)}, u32[]{:S(2)}) collective-permute-start(bf16[256,1024]{1,0:T(8,128)(2,1)} %bitcast.38), channel_id=1, source_target_pairs={{0,1},{1,2},{2,3},{3,4},{4,5},{5,6},{6,7},{7,8},{8,9},{9,10},{10,1... | collective-permute-start | bytes 1572872 | tf_op jit(solution)/shard_map/ppermute | solution.py:58
  27.4 28.7 %collective-permute-start.5 = (bf16[256,1024]{1,0:T(8,128)(2,1)}, bf16[256,1024]{1,0:T(8,128)(2,1)}, u32[]{:S(2)}, u32[]{:S(2)}) collective-permute-start(bf16[256,1024]{1,0:T(8,128)(2,1)} %bitcast.39), channel_id=1, source_target_pairs={{1,0},{2,1},{3,2},{4,3},{5,4},{6,5},{7,6},{8,7},{9,8},{10,9},{11,1... | collective-permute-start | bytes 1572872 | tf_op jit(solution)/shard_map/ppermute | solution.py:58
  46.0 11.7 %collective-permute-start.2 = (bf16[256,218]{1,0:T(8,128)(2,1)S(1)}, bf16[256,218]{1,0:T(8,128)(2,1)S(1)}, u32[]{:S(2)}, u32[]{:S(2)}) collective-permute-start(bf16[256,218]{1,0:T(8,128)(2,1)S(1)} %pooled.1.pool_own), channel_id=1, source_target_pairs={{0,1},{1,2},{2,3},{3,4},{4,5},{5,6},{6,7},{7,8},{8,9},{9,10},{10,1... | collective-permute-start | bytes 334856 | tf_op jit(solution)/shard_map/ppermute | solution.py:58
  47.9 11.0 %collective-permute-start.3 = (bf16[256,218]{1,0:T(8,128)(2,1)S(1)}, bf16[256,218]{1,0:T(8,128)(2,1)S(1)}, u32[]{:S(2)}, u32[]{:S(2)}) collective-permute-start(bf16[256,218]{1,0:T(8,128)(2,1)S(1)} %pooled.1.pool_own), channel_id=1, source_target_pairs={{1,0},{2,1},{3,2},{4,3},{5,4},{6,5},{7,6},{8,7},{9,8},{10,9},{11,1... | collective-permute-start | bytes 334856 | tf_op jit(solution)/shard_map/ppermute | solution.py:58
  56.1 10.7 %copy-start.2 = (bf16[1024,1024]{1,0:T(8,128)(2,1)S(1)}, bf16[1024,1024]{1,0:T(8,128)(2,1)}, u32[]{:S(2)}) copy-start(bf16[1024,1024]{1,0:T(8,128)(2,1)} %out_hbm.1) | copy-start | bytes 6291460
  78.7 2.0 %collective-permute-start.6 = (bf16[256,1024]{1,0:T(8,128)(2,1)S(1)}, bf16[256,1024]{1,0:T(8,128)(2,1)S(1)}, u32[]{:S(2)}, u32[]{:S(2)}) collective-permute-start(bf16[256,1024]{1,0:T(8,128)(2,1)S(1)} %get-tuple-element.14.tokens_ref), channel_id=1, source_target_pairs={{0,64},{64,0},{1,65},{65,1},{2,66},{66,2},{3,67},{67,3},{4,68},{68... | collective-permute-start | bytes 1572872 | tf_op jit(solution)/shard_map/ppermute | solution.py:62
  117.4 3.4 %copy-start = (bf16[64,32,2048]{2,1,0:T(8,128)(2,1)S(1)}, bf16[64,32,2048]{2,1,0:T(8,128)(2,1)}, u32[]{:S(2)}) copy-start(bf16[64,32,2048]{2,1,0:T(8,128)(2,1)} %all-gather.4.cloned.1.call-done) | copy-start | bytes 25165828
  120.8 4.6 %copy-start.1 = (bf16[64,32,2048]{2,1,0:T(8,128)(2,1)S(1)}, bf16[64,32,2048]{2,1,0:T(8,128)(2,1)}, u32[]{:S(2)}) copy-start(bf16[64,32,2048]{2,1,0:T(8,128)(2,1)} %all-gather.4.cloned.1.call-done) | copy-start | bytes 25165828
  125.3 4.7 %copy-start.5 = (bf16[1024,100]{0,1:T(8,128)(2,1)S(1)}, bf16[1024,100]{0,1:T(8,128)(2,1)}, u32[]{:S(2)}) copy-start(bf16[1024,100]{0,1:T(8,128)(2,1)} %param.27) | copy-start | bytes 614404
  125.3 4.7 %collective-permute-start.7 = (f32[256,1024]{1,0:T(8,128)S(1)}, f32[256,1024]{1,0:T(8,128)S(1)}, u32[]{:S(2)}, u32[]{:S(2)}) collective-permute-start(f32[256,1024]{1,0:T(8,128)S(1)} %mlp_part.3), channel_id=1, source_target_pairs={{0,64},{64,0},{1,65},{65,1},{2,66},{66,2},{3,67},{67,3},{4,68},{68... | collective-permute-start | bytes 3145736 | tf_op jit(solution)/shard_map/ppermute | solution.py:62
  129.9 6.6 %copy-start.9 = (s32[1024,4]{0,1:T(4,128)S(1)}, s32[1024,4]{0,1:T(4,128)}, u32[]{:S(2)}) copy-start(s32[1024,4]{0,1:T(4,128)} %param.19) | copy-start | bytes 49156
  130.0 31.5 %copy-start.4 = (bf16[100,1024]{1,0:T(8,128)(2,1)S(1)}, bf16[100,1024]{1,0:T(8,128)(2,1)}, u32[]{:S(2)}) copy-start(bf16[100,1024]{1,0:T(8,128)(2,1)} %truth_ref.1) | copy-start | bytes 614404
  130.6 1.5 collective-permute-start.8
  132.1 20.5 %collective-permute-start.13 = (bf16[2,100,256]{2,1,0:T(8,128)(2,1)S(1)}, bf16[2,100,256]{2,1,0:T(8,128)(2,1)S(1)}, u32[]{:S(2)}, u32[]{:S(2)}) collective-permute-start(bf16[2,100,256]{2,1,0:T(8,128)(2,1)S(1)} %pad_maximum_fusion.1), channel_id=1, source_target_pairs={{1,128},{2,129},{3,130},{4,131},{5,132},{6,133},{7,134},{8,135},{9... | collective-permute-start | bytes 307208 | tf_op jit(solution)/shard_map/ppermute | solution.py:447
  137.9 14.8 %collective-permute-start.12 = (bf16[2,100,256]{2,1,0:T(8,128)(2,1)S(1)}, bf16[2,100,256]{2,1,0:T(8,128)(2,1)S(1)}, u32[]{:S(2)}, u32[]{:S(2)}) collective-permute-start(bf16[2,100,256]{2,1,0:T(8,128)(2,1)S(1)} %pad_maximum_fusion.1), channel_id=1, source_target_pairs={{0,128},{1,129},{2,130},{3,131},{4,132},{5,133},{6,134},{7,135},{8... | collective-permute-start | bytes 307208 | tf_op jit(solution)/shard_map/ppermute | solution.py:447
  139.1 13.6 %collective-permute-start.11 = (bf16[2,100,256]{2,1,0:T(8,128)(2,1)S(1)}, bf16[2,100,256]{2,1,0:T(8,128)(2,1)S(1)}, u32[]{:S(2)}, u32[]{:S(2)}) collective-permute-start(bf16[2,100,256]{2,1,0:T(8,128)(2,1)S(1)} %pad_maximum_fusion.1), channel_id=1, source_target_pairs={{0,129},{1,130},{2,131},{3,132},{4,133},{5,134},{6,135},{7,136},{8... | collective-permute-start | bytes 307208 | tf_op jit(solution)/shard_map/ppermute | solution.py:447
  143.8 9.1 %collective-permute-start.10 = (bf16[2,100,256]{2,1,0:T(8,128)(2,1)S(1)}, bf16[2,100,256]{2,1,0:T(8,128)(2,1)S(1)}, u32[]{:S(2)}, u32[]{:S(2)}) collective-permute-start(bf16[2,100,256]{2,1,0:T(8,128)(2,1)S(1)} %pad_maximum_fusion.1), channel_id=1, source_target_pairs={{1,0},{2,1},{3,2},{4,3},{5,4},{6,5},{7,6},{8,7},{9,8},{10,9},{11,1... | collective-permute-start | bytes 307208 | tf_op jit(solution)/shard_map/ppermute | solution.py:447
  150.7 10.8 %collective-permute-start.9 = (bf16[2,100,256]{2,1,0:T(8,128)(2,1)S(1)}, bf16[2,100,256]{2,1,0:T(8,128)(2,1)S(1)}, u32[]{:S(2)}, u32[]{:S(2)}) collective-permute-start(bf16[2,100,256]{2,1,0:T(8,128)(2,1)S(1)} %pad_maximum_fusion.1), channel_id=1, source_target_pairs={{0,1},{1,2},{2,3},{3,4},{4,5},{5,6},{6,7},{7,8},{8,9},{9,10},{10,1... | collective-permute-start | bytes 307208 | tf_op jit(solution)/shard_map/ppermute | solution.py:447
Sparse Core Ops, SparseCore 0:
  13.8 103.5 all-gather.3

commit v2 on v1

--- a/solution.py
+++ b/solution.py
@@ -1,5 +1,3 @@
-import functools
-
 import jax
 import jax.numpy as jnp
 from jax import lax
@@ -62,53 +60,55 @@
     return lax.ppermute(block, "member_core", [(0, 1), (1, 0)])
 
 
-def tally_kernel(slots_ref, out_ref):
-    rows = 16
-    width = out_ref.shape[1]
-    chunk = 1024
+def tally_kernel(place_ref, slots_ref, count_ref, out_ref):
+    rows = 64
+    nodes = out_ref.shape[1]
+    slots = slots_ref[...] - place_ref[2]
+    used = lax.broadcasted_iota(jnp.int32, slots.shape, 0) < count_ref[...]
+    slots = jnp.where(used, slots, -1)
 
     def body(step, carry):
         first = pl.multiple_of(step * rows, rows)
-        slots = slots_ref[pl.ds(first, rows), :]
-        for start in range(0, width, chunk):
-            window = lax.broadcasted_iota(jnp.int32, (rows, chunk), 1) + start
-            total = jnp.zeros((rows, chunk), F32)
-            for position in range(slots.shape[1]):
-                hit = slots[:, position : position + 1] == window
-                total = total + jnp.where(hit, 1.0, 0.0)
-            out_ref[pl.ds(first, rows), start : start + chunk] = total.astype(BF16)
+        window = first + lax.broadcasted_iota(jnp.int32, (rows, nodes), 0)
+        total = jnp.zeros((rows, nodes), F32)
+        for position in range(slots.shape[0]):
+            hit = slots[position : position + 1, :] == window
+            total = total + jnp.where(hit, 1.0, 0.0)
+        out_ref[pl.ds(first, rows), :] = total.astype(BF16)
         return carry
 
     lax.fori_loop(0, out_ref.shape[0] // rows, body, 0)
 
 
-def encoder_tallies(slots, width):
-    nodes, count = slots.shape
+def encoder_tallies(place, slots, counts, width):
+    count, nodes = slots.shape
+    vmem = pl.BlockSpec(memory_space=pltpu.VMEM)
     return pl.pallas_call(
         tally_kernel,
-        out_shape=jax.ShapeDtypeStruct((nodes, width), BF16),
+        out_shape=jax.ShapeDtypeStruct((width, nodes), BF16),
+        in_specs=[pl.BlockSpec(memory_space=pltpu.SMEM), vmem, vmem],
         compiler_params=params(16),
         cost_estimate=cost(3 * nodes * width * count, nodes * width * 2),
         name="encoder_tallies",
-    )(slots)
+    )(place, slots, counts)
 
 
 def pooled_kernel(tally_ref, low_ref, own_ref, high_ref, count_ref, out_ref):
     width = low_ref.shape[1]
-    total = dot_lanes(tally_ref[:, width : 2 * width], own_ref[...])
-    total = total + dot_lanes(tally_ref[:, :width], low_ref[...])
-    total = total + dot_lanes(tally_ref[:, 2 * width :], high_ref[...])
-    out_ref[...] = (total / count_ref[...]).astype(BF16)
+    total = dot(own_ref[...], tally_ref[width : 2 * width, :])
+    total = total + dot(low_ref[...], tally_ref[:width, :])
+    total = total + dot(high_ref[...], tally_ref[2 * width :, :])
+    out_ref[...] = (total / count_ref[...].astype(F32)).astype(BF16)
 
 
 def pool(tallies, low, own, high, counts):
-    nodes = tallies.shape[0]
+    nodes = tallies.shape[1]
     channels = own.shape[0]
     return pl.pallas_call(
         pooled_kernel,
-        out_shape=jax.ShapeDtypeStruct((nodes, channels), BF16),
+        out_shape=jax.ShapeDtypeStruct((channels, nodes), BF16),
         compiler_params=params(24),
-        cost_estimate=cost(2 * nodes * tallies.shape[1] * channels, tallies.size * 4),
+        cost_estimate=cost(2 * tallies.size * channels, tallies.size * 4),
         name="pooled",
     )(tallies, low, own, high, counts)
 
@@ -123,7 +123,10 @@
     gain = gain_ref[0:1, :]
 
     def start_of(pooled, perturb):
-        return dot(pooled[...], embed_ref[...]) + perturb[...].astype(F32)
+        embedded = lax.dot_general(
+            pooled[...], embed_ref[...], (((0,), (0,)), ((), ())), preferred_element_type=F32
+        )
+        return embedded + perturb[...].astype(F32)
 
     normed = []
     for place, (pooled, perturb) in enumerate(
@@ -173,10 +176,11 @@
     span = cap_ref.shape[2]
     first_query = where_ref[0]
     node_total = where_ref[1]
+    reaches = jnp.transpose(jnp.broadcast_to(reach_ref[...].astype(F32), (128, nodes)))
     for block in range(nodes // rows):
         at = first_query + block * rows + lax.broadcasted_iota(jnp.int32, (rows, span), 0)
         key = first_query - BAND + block * rows + lax.broadcasted_iota(jnp.int32, (rows, span), 1)
-        reach = reach_ref[block * rows : (block + 1) * rows, :]
+        reach = reaches[block * rows : (block + 1) * rows, :1].astype(jnp.int32)
         allowed = (jnp.abs(at - key) <= reach) & (key >= 0) & (key < node_total)
         cap_ref[block] = jnp.where(allowed, 3e38, -1e30)
 
@@ -238,50 +242,129 @@
     )(where, query, kv, reach, start, norm_gains, out_weight)
 
 
-def mlp_kernel(tokens_ref, weight_ref, out_ref):
-    blocks, sides, rows, columns = weight_ref.shape
-    rows = rows // 2
-    part = blocks * rows
-
-    upper = None
-    for side in range(sides):
-        up = weight_ref[:, side, :rows, :].reshape(part, columns)
-        term = dot(tokens_ref[:, side * part : (side + 1) * part], up)
-        upper = term if upper is None else upper + term
-    active = jax.nn.gelu(upper).astype(BF16)
-    lowered = []
-    for side in range(sides):
-        down = weight_ref[:, side, rows:, :].reshape(part, columns)
-        lowered.append(dot_lanes(active, down))
-
-    @pl.when(pl.program_id(0) == 0)
-    def _():
-        for side in range(sides):
-            out_ref[:, side * part : (side + 1) * part] = lowered[side]
-
-    @pl.when(pl.program_id(0) > 0)
-    def _():
-        for side in range(sides):
-            out_ref[:, side * part : (side + 1) * part] += lowered[side]
-
-
-def mlp_part(tokens, weights):
-    nodes, width = tokens.shape
-    blocks, sides, rows, hidden = weights.shape
+def in_order_kernel(place_ref, *refs):
+    out_ref = refs[-1]
+    count = len(refs) - 1
+    for shift in range(count):
+        out_ref[lax.rem(place_ref[4] + shift, count)] = refs[shift][...]
+
+
+def in_order(place, blocks):
+    count = len(blocks)
+    vmem = pl.BlockSpec(memory_space=pltpu.VMEM)
+    return pl.pallas_call(
+        in_order_kernel,
+        out_shape=jax.ShapeDtypeStruct((count,) + blocks[0].shape, BF16),
+        in_specs=[pl.BlockSpec(memory_space=pltpu.SMEM)] + [vmem] * count,
+        compiler_params=params(16),
+        cost_estimate=cost(0, 2 * count * blocks[0].size * 2),
+        name="shards_in_order",
+    )(place, *blocks)
+
+
+def mlp_kernel(place_ref, own_ref, other_ref, *refs):
+    blocks = refs[:8]
+    far = refs[8:10]
+    own_out, other_out, tokens_ref, total_ref = refs[10:]
+    nodes, width = own_ref.shape
+    part = width // 8
+    hidden = blocks[0].shape[2]
+    rows = blocks[0].shape[1] // 2
     step = 512
+
+    def at(block):
+        along_x = lax.rem(place_ref[3] + (0, 3, 1, 2)[block % 4], 4)
+        along_y = place_ref[5] if block < 4 else 1 - place_ref[5]
+        return pl.ds(pl.multiple_of((along_y * 4 + along_x) * part, part), part)
+
+    for block in range(8):
+        columns = slice(block * part, (block + 1) * part)
+        tokens_ref[:nodes, columns] = other_ref[:, at(block)]
+        tokens_ref[nodes:, columns] = own_ref[:, at(block)]
+
+    def all_rows(first, chosen):
+        pieces = []
+        for block in range(8):
+            if block % 4 < 3:
+                sources = (blocks[block - block // 4],)
+            else:
+                sources = ((blocks[6], blocks[7]), far)[block // 4]
+            for source in sources:
+                piece = source[:, first : first + rows, chosen]
+                pieces.append(piece.reshape(piece.shape[0] * rows, step))
+        return jnp.concatenate(pieces, axis=0)
+
+    for start in range(0, hidden, step):
+        chosen = slice(start, start + step)
+        upper = dot(tokens_ref[...], all_rows(0, chosen))
+        active = jax.nn.gelu(upper).astype(BF16)
+        lowered = dot_lanes(active, all_rows(rows, chosen))
+        if start == 0:
+            total_ref[...] = lowered
+        else:
+            total_ref[...] += lowered
+    for block in range(8):
+        columns = slice(block * part, (block + 1) * part)
+        other_out[:, at(block)] = total_ref[:nodes, columns]
+        own_out[:, at(block)] = total_ref[nodes:, columns]
+
+
+def mlp_parts(place, own, other, blocks):
+    nodes, width = own.shape
+    hidden = blocks[0].shape[2]
+    vmem = pl.BlockSpec(memory_space=pltpu.VMEM)
     return pl.pallas_call(
         mlp_kernel,
-        grid=(hidden // step,),
-        out_shape=jax.ShapeDtypeStruct((nodes, width), F32),
-        in_specs=[
-            pl.BlockSpec((nodes, width), lambda j: (0, 0)),
-            pl.BlockSpec((blocks, sides, rows, step), lambda j: (0, 0, 0, j)),
+        out_shape=(jax.ShapeDtypeStruct((nodes, width), F32),) * 2,
+        in_specs=[pl.BlockSpec(memory_space=pltpu.SMEM)] + [vmem] * (2 + len(blocks)),
+        scratch_shapes=[
+            pltpu.VMEM((2 * nodes, width), BF16),
+            pltpu.VMEM((2 * nodes, width), F32),
         ],
-        out_specs=pl.BlockSpec((nodes, width), lambda j: (0, 0)),
-        compiler_params=params(32),
-        cost_estimate=cost(4 * nodes * width * hidden, weights.size * 2, nodes * hidden),
-        name="mlp_part",
-    )(tokens, weights)
+        compiler_params=params(40),
+        cost_estimate=cost(8 * nodes * width * hidden, 12 << 20, 2 * nodes * hidden),
+        name="mlp_parts",
+    )(place, own, other, *blocks)
+
+
+def gathered_shards(place, share):
+    def turn(block, axis, step):
+        count = lax.axis_size(axis)
+        return lax.ppermute(block, axis, [(i, (i + step) % count) for i in range(count)])
+
+    def beside(block):
+        return lax.ppermute(block, NODE[0], [(0, 1), (1, 0)])
+
+    def across(block):
+        return lax.ppermute(
+            block, (MEMBER[0], NODE[0]), [(0, 3), (3, 0), (1, 2), (2, 1)]
+        )
+
+    ahead, behind = [share], [share]
+    for step in range(4):
+        ahead.append(turn(ahead[-1], NODE[2], 1))
+        if step < 3:
+            behind.append(turn(behind[-1], NODE[2], -1))
+    column = in_order(
+        place, [share] + behind[1:] + [ahead[4], ahead[3], ahead[2], ahead[1]]
+    )
+    before = turn(column, NODE[1], 1)
+    after = turn(column, NODE[1], -1)
+    half = column.shape[0] // 2
+    far_low = turn(before[:half], NODE[1], 1)
+    far_high = turn(after[half:], NODE[1], -1)
+    return (
+        column,
+        before,
+        after,
+        beside(column),
+        beside(before),
+        across(after),
+        far_low,
+        far_high,
+        beside(far_low),
+        across(far_high),
+    )
 
 
 def head_kernel(mid_ref, own_ref, other_ref, gain_ref, head_ref, out_ref):
@@ -302,14 +385,14 @@
     )(middle, own, other, norm_gains, head_rows)
 
 
-def decoder_tally_kernel(slots_ref, out_ref):
+def decoder_tally_kernel(place_ref, slots_ref, out_ref):
     rows = 64
     points = out_ref.shape[1]
     slots = slots_ref.shape[0]
 
     def body(step, carry):
         first = pl.multiple_of(step * rows, rows)
-        node = first + lax.broadcasted_iota(jnp.int32, (rows, points), 0)
+        node = first + place_ref[7] + lax.broadcasted_iota(jnp.int32, (rows, points), 0)
         total = jnp.zeros((rows, points), F32)
         for position in range(slots):
             hit = slots_ref[position : position + 1, :] == node
@@ -320,52 +403,51 @@
     lax.fori_loop(0, out_ref.shape[0] // rows, body, 0)
 
 
-def decoder_tallies(slots, nodes):
+def decoder_tallies(place, slots, nodes):
     count, points = slots.shape
     return pl.pallas_call(
         decoder_tally_kernel,
+        in_specs=[
+            pl.BlockSpec(memory_space=pltpu.SMEM),
+            pl.BlockSpec(memory_space=pltpu.VMEM),
+        ],
         out_shape=jax.ShapeDtypeStruct((nodes, points), BF16),
         compiler_params=params(16),
         cost_estimate=cost(3 * nodes * points * count, nodes * points * 2),
         name="decoder_tallies",
-    )(slots)
-
-
-def crps_kernel(tally_ref, state_ref, truth_ref, *refs):
-    out_ref = refs[-1]
-    refs = refs[:-1]
-    variables = out_ref.shape[0]
-    nodes = refs[0].shape[1]
+    )(place, slots)
+
+
+def crps_kernel(place_ref, tally_ref, state_ref, truth_ref, low_ref, own_ref, high_ref, out_ref, field_ref):
+    members, variables, nodes = own_ref.shape
     state = state_ref[:variables, :].astype(F32)
-    forecasts = []
-    for member in range(len(refs) // 3):
-        field = None
-        for place in range(3):
-            term = dot(
-                refs[3 * member + place][...], tally_ref[place * nodes : (place + 1) * nodes, :]
-            )
-            field = term if field is None else field + term
-        forecasts.append(state + field)
-    members = len(forecasts)
-    own = forecasts[0]
+    for member in range(members):
+        field = dot(own_ref[member], tally_ref[nodes : 2 * nodes, :])
+        field = field + dot(low_ref[member], tally_ref[:nodes, :])
+        field = field + dot(high_ref[member], tally_ref[2 * nodes :, :])
+        field_ref[member] = state + field
+    own = field_ref[place_ref[6]]
     pairwise = None
-    for other in forecasts:
-        term = score_gradient(own - other)
+    for member in range(members):
+        term = score_gradient(own - field_ref[member])
         pairwise = term if pairwise is None else pairwise + term
-    out_ref[...] = score_gradient(own - truth_ref[...].astype(F32)) * (
+    out_ref[0] = score_gradient(own - truth_ref[...].astype(F32)) * (
         1.0 / members
     ) - pairwise * (1.0 / (members * (members - 1)))
 
 
-def crps(tallies, state, truth, projected):
+def crps(place, tallies, state, truth, low, own, high):
     variables, points = truth.shape
+    vmem = pl.BlockSpec(memory_space=pltpu.VMEM)
     return pl.pallas_call(
         crps_kernel,
-        out_shape=jax.ShapeDtypeStruct((variables, points), F32),
+        out_shape=jax.ShapeDtypeStruct((1, variables, points), F32),
+        in_specs=[pl.BlockSpec(memory_space=pltpu.SMEM)] + [vmem] * 6,
+        scratch_shapes=[pltpu.VMEM((own.shape[0], variables, points), F32)],
         compiler_params=params(32),
         cost_estimate=cost(2 * 4 * variables * points * tallies.shape[0], 4 << 20),
         name="decoder_crps",
-    )(tallies, state, truth, *projected)
+    )(place, tallies, state, truth, low, own, high)
 
 
 def per_device(
@@ -392,6 +474,21 @@
     hidden = up_weight.shape[1] // 2
     perturb = member_perturb[0]
 
+    place = jnp.stack(
+        [
+            region * node_dev,
+            region_count * node_dev,
+            (region - 1) * grid_dev,
+            lax.axis_index(NODE[1]),
+            lax.axis_index(NODE[2]),
+            lax.axis_index(NODE[0]),
+            lax.axis_index(MEMBER),
+            (region - 1) * node_dev,
+        ]
+    ).astype(jnp.int32)
+
+    state_low, state_high = neighbours(gridpoint_state)
+
     share = jnp.concatenate(
         [
             lax.dynamic_slice_in_dim(up_weight, core * hidden, hidden, 1),
@@ -399,22 +496,12 @@
         ],
         axis=0,
     )
-    pair = lax.all_gather(share, NODE[0], axis=0)
-    weights = lax.all_gather(pair, NODE[1:], axis=0)
-
-    state_low, state_high = neighbours(gridpoint_state)
+    shards = gathered_shards(place, share)
     perturb_low, perturb_high = neighbours(perturb)
 
-    positions = jnp.arange(encoder_slots.shape[1], dtype=jnp.int32)
-    local_slots = jnp.where(
-        positions[None, :] < encoder_count[:, None],
-        encoder_slots - (region - 1) * grid_dev,
-        -1,
-    )
-    tallies = encoder_tallies(local_slots, 3 * grid_dev)
-    near_slots = (decoder_slots - (region - 1) * node_dev).T
-    decoder_near = decoder_tallies(near_slots, 3 * node_dev)
-    counts = encoder_count[:, None].astype(F32)
+    counts = encoder_count[None, :]
+    tallies = encoder_tallies(place, encoder_slots.T, counts, 3 * grid_dev)
+    decoder_near = decoder_tallies(place, decoder_slots.T, 3 * node_dev)
     pooled = pool(tallies, state_low, gridpoint_state, state_high, counts)
     pooled_low, pooled_high = neighbours(pooled)
     start, query, kv = qkv(
@@ -424,36 +511,25 @@
         norm_gains,
         qkv_weight,
     )
-    where = jnp.stack([region * node_dev, jnp.int32(region_count * node_dev)])
     middle, normed_mid = attention(
-        where, query, kv, node_reach[:, None], start, norm_gains, out_weight
+        place, query, kv, node_reach[None, :], start, norm_gains, out_weight
     )
 
     normed_other = other_core(normed_mid)
-    part_other = mlp_part(normed_other, weights)
-    part_mine = mlp_part(normed_mid, weights)
+    part_mine, part_other = mlp_parts(place, normed_mid, normed_other, shards)
     projected = head(middle, part_mine, other_core(part_other), norm_gains, head_weight.T)
 
-    both = jnp.stack([projected, other_core(projected)])
-    axes = ("member_hi",) + NODE
-    def sent(step, flip):
-        links = []
-        for side in range(2):
-            for i in range(region_count):
-                j = i + step
-                if 0 <= j < region_count:
-                    target = (1 - side) if flip else side
-                    links.append((side * region_count + i, target * region_count + j))
-        return lax.ppermute(both, axes, links)
-
-    low, high = sent(1, False), sent(-1, False)
-    far_low, far_own, far_high = sent(1, True), sent(0, True), sent(-1, True)
-    projected_all = []
-    for near in ((low, both, high), (far_low, far_own, far_high)):
-        for k in range(2):
-            projected_all += [block[k] for block in near]
-    gradient = crps(decoder_near, gridpoint_state, grid_truth, projected_all)
-    return gradient[None]
+    projected_all = lax.all_gather(projected, MEMBER, axis=0)
+    projected_low, projected_high = neighbours(projected_all)
+    return crps(
+        place,
+        decoder_near,
+        gridpoint_state,
+        grid_truth,
+        projected_low,
+        projected_all,
+        projected_high,
+    )
 
 
 def solution(mesh):

time: 171 us -> 186 us (1.088)
  waiting for transfers between devices: 51 us -> 76 us
  between operations: 13.8 us -> 0.41 us
  starting transfers between devices: 51.9 us -> 61.8 us
  Pallas kernels: 39.1 us -> 36.1 us
  local copies, waits for them, and re-layouts: 6.63 us -> 3.73 us
  other arithmetic: 2.29 us -> 0.01 us
    ppermute x5 -> x16, waiting for transfers between devices: 8.8 us -> 70.4 us  [the longest x3 40.5 us: beside(): return lax.ppermute(block, NODE[0], [(0, 1), (1, 0)])]
    all_gather x1 -> x0, waiting for transfers between devices: 36.7 us -> none  [per_device(): weights = lax.all_gather(pair, NODE[1:], axis=0)]
    ppermute x3 -> x4, starting transfers between devices: 24.2 us -> 31.6 us  [neighbours(): lax.ppermute(block, NODE, backward)]
    ppermute x5 -> x16, starting transfers between devices: 19.2 us -> 22.3 us  [the longest x11 15.9 us: turn(): lax.ppermute(block, axis, [(i, (i + step) % count) for i in range(count)])]
    broadcast_in_dim x2 -> x0, local copies, waits for them, and re-layouts: 1.99 us -> none  [the longest x1 1.17 us: per_device(): return gradient[None]]
    unnamed x20 -> x24, local copies, waits for them, and re-layouts: 3.43 us -> 1.46 us
    ppermute x3 -> x4, starting transfers between devices: 7.67 us -> 7.66 us  [neighbours(): lax.ppermute(block, NODE, forward)]
  transfers between devices with their start and end apart: 15 -> 26, of which waited for: 7 -> 9; matrix products, arithmetic and copies ran while one was open for 2% -> 0% of each run, Pallas kernels for 19% -> 15%
where the time goes in v2:
time: 186 us; the launch traced here: 185 us
  waiting for transfers between devices  76 us (41%)
  starting transfers between devices  61.8 us (33%)
  Pallas kernels  36.1 us (19%)
  blocking collectives  7.16 us (4%)
  local copies, waits for them, and re-layouts  3.73 us (2%)
    ppermute x3, waiting for transfers between devices, beside(): return lax.ppermute(block, NODE[0], [(0, 1), (1, 0)])  40.5 us
    ppermute x4, starting transfers between devices, neighbours(): lax.ppermute(block, NODE, backward)  31.6 us
    ppermute x11, waiting for transfers between devices, turn(): lax.ppermute(block, axis, [(i, (i + step) % count) for i in range(count)])  30 us
    ppermute x11, starting transfers between devices, turn(): lax.ppermute(block, axis, [(i, (i + step) % count) for i in range(count)])  15.9 us
    pallas_call x1, Pallas kernels, attention(): pl.pallas_call(attention_kernel, out_shape=(jax.ShapeDtypeStruct((nodes,...  11.7 us
    ppermute x4, starting transfers between devices, neighbours(): lax.ppermute(block, NODE, forward)  7.66 us
    all_gather x1, blocking collectives, per_device(): projected_all = lax.all_gather(projected, MEMBER, axis=0)  7.16 us
    pallas_call x1, Pallas kernels, qkv(): pl.pallas_call(qkv_kernel, out_shape=(jax.ShapeDtypeStruct((nodes, width)...  6.76 us
  transfers between devices with their start and end apart: 26, of which 9 were waited for; matrix products, arithmetic and copies ran while one was open for 0% of the time, Pallas kernels for 15%

profile of v2, /device:TPU:8, one launch (start us, length us, event | category | flops | bytes accessed | tf_op | source)
XLA Modules:
  0.0 185.3 jit_solution(13832635710299991102)
XLA Ops:
  0.0 0.9 constant_dynamic-slice_fusion
  1.0 2.0 %collective-permute-start.10 = (bf16[32,2048]{1,0:T(8,128)(2,1)S(1)}, bf16[32,2048]{1,0:T(8,128)(2,1)S(1)}, u32[]{:S(2)}, u32[]{:S(2)}) collective-permute-start(bf16[32,2048]{1,0:T(8,128)(2,1)S(1)} %pad_maximum_fusion.refs_0_), channel_id=1, source_target_pairs={{0,1},{1,2},{2,3},{3,4},{4,5},{5,6},{6,7},{7,0},{8,9},{9,10},{10,1... | collective-permute-start | bytes 393224 | tf_op jit(solution)/shard_map/ppermute | solution.py:333
  3.0 4.0 %collective-permute-start.7 = (bf16[32,2048]{1,0:T(8,128)(2,1)S(1)}, bf16[32,2048]{1,0:T(8,128)(2,1)S(1)}, u32[]{:S(2)}, u32[]{:S(2)}) collective-permute-start(bf16[32,2048]{1,0:T(8,128)(2,1)S(1)} %pad_maximum_fusion.refs_0_), channel_id=1, source_target_pairs={{0,7},{1,0},{2,1},{3,2},{4,3},{5,4},{6,5},{7,6},{8,15},{9,8},{10,9... | collective-permute-start | bytes 393224 | tf_op jit(solution)/shard_map/ppermute | solution.py:333
  7.0 1.9 %collective-permute-start = (bf16[218,1024]{1,0:T(8,128)(2,1)}, bf16[218,1024]{1,0:T(8,128)(2,1)S(1)}, u32[]{:S(2)}, u32[]{:S(2)}) collective-permute-start(bf16[218,1024]{1,0:T(8,128)(2,1)} %state_ref.1), channel_id=1, source_target_pairs={{0,1},{1,2},{2,3},{3,4},{4,5},{5,6},{6,7},{7,8},{8,9},{9,10},{10,1... | collective-permute-start | bytes 1339400 | tf_op jit(solution)/shard_map/ppermute | solution.py:56
  8.9 1.5 collective-permute-done.10.refs_7_
  10.4 0.0 collective-permute-start.11
  10.4 7.2 %collective-permute-start.1 = (bf16[218,1024]{1,0:T(8,128)(2,1)}, bf16[218,1024]{1,0:T(8,128)(2,1)S(1)}, u32[]{:S(2)}, u32[]{:S(2)}) collective-permute-start(bf16[218,1024]{1,0:T(8,128)(2,1)} %state_ref.1), channel_id=1, source_target_pairs={{1,0},{2,1},{3,2},{4,3},{5,4},{6,5},{7,6},{8,7},{9,8},{10,9},{11,1... | collective-permute-start | bytes 1339400 | tf_op jit(solution)/shard_map/ppermute | solution.py:56
  17.6 1.9 %collective-permute-start.4 = (bf16[256,1024]{1,0:T(8,128)(2,1)}, bf16[256,1024]{1,0:T(8,128)(2,1)S(1)}, u32[]{:S(2)}, u32[]{:S(2)}) collective-permute-start(bf16[256,1024]{1,0:T(8,128)(2,1)} %bitcast.21), channel_id=1, source_target_pairs={{0,1},{1,2},{2,3},{3,4},{4,5},{5,6},{6,7},{7,8},{8,9},{9,10},{10,1... | collective-permute-start | bytes 1572872 | tf_op jit(solution)/shard_map/ppermute | solution.py:56
  19.5 0.0 collective-permute-done.7.refs_1_
  19.6 8.1 %collective-permute-start.5 = (bf16[256,1024]{1,0:T(8,128)(2,1)}, bf16[256,1024]{1,0:T(8,128)(2,1)S(1)}, u32[]{:S(2)}, u32[]{:S(2)}) collective-permute-start(bf16[256,1024]{1,0:T(8,128)(2,1)} %bitcast.22), channel_id=1, source_target_pairs={{1,0},{2,1},{3,2},{4,3},{5,4},{6,5},{7,6},{8,7},{9,8},{10,9},{11,1... | collective-permute-start | bytes 1572872 | tf_op jit(solution)/shard_map/ppermute | solution.py:56
  27.7 0.0 collective-permute-done.11.refs_6_
  27.7 0.1 collective-permute-start.8
  27.8 13.0 %collective-permute-done.8.refs_2_ = bf16[32,2048]{1,0:T(8,128)(2,1)S(1)} collective-permute-done((bf16[32,2048]{1,0:T(8,128)(2,1)S(1)}, bf16[32,2048]{1,0:T(8,128)(2,1)S(1)}, u32[]{:S(2)}, u32[]{:S(2)}) %collective-permute-start.8) | collective-permute-done | bytes 131104 | tf_op jit(solution)/shard_map/ppermute | solution.py:333
  40.8 6.6 %collective-permute-done.12.refs_5_ = bf16[32,2048]{1,0:T(8,128)(2,1)S(1)} collective-permute-done((bf16[32,2048]{1,0:T(8,128)(2,1)S(1)}, bf16[32,2048]{1,0:T(8,128)(2,1)S(1)}, u32[]{:S(2)}, u32[]{:S(2)}) %collective-permute-start.12) | collective-permute-done | bytes 131104 | tf_op jit(solution)/shard_map/ppermute | solution.py:333
  47.4 3.1 %collective-permute-start.9 = (bf16[32,2048]{1,0:T(8,128)(2,1)S(1)}, bf16[32,2048]{1,0:T(8,128)(2,1)S(1)}, u32[]{:S(2)}, u32[]{:S(2)}) collective-permute-start(bf16[32,2048]{1,0:T(8,128)(2,1)S(1)} %collective-permute-done.8.refs_2_), channel_id=1, source_target_pairs={{0,7},{1,0},{2,1},{3,2},{4,3},{5,4},{6,5},{7,6},{8,15},{9,8},{10,9... | collective-permute-start | bytes 393224 | tf_op jit(solution)/shard_map/ppermute | solution.py:333
  50.6 0.1 stack.31.place_ref.where_ref
  50.6 0.7 copy-done.5
  51.4 0.7 copy-done.7
  52.0 6.0 %encoder_tallies.1.tally_ref = bf16[3072,256]{1,0:T(8,128)(2,1)S(1)} custom-call(s32[8]{0:T(128)S(1)} %stack.31.place_ref.where_ref, s32[16,256]{1,0:T(8,128)S(1)} %bitcast.16, s32[1,256]{1,0:T(1,128)S(1)} %bitcast.18), custom_call_target="tpu_custom_call" | custom-call | flops 37748736 | bytes 1572864 | tf_op jit(solution)/shard_map/encoder_tallies/pallas_call | solution.py:86
  58.0 0.0 copy-start.4
  58.0 0.0 copy-start.10
  58.1 0.0 copy-start.11
  58.1 0.5 pooled.1.pool_own
  58.6 1.9 %collective-permute-start.2 = (bf16[218,256]{1,0:T(8,128)(2,1)S(1)}, bf16[218,256]{1,0:T(8,128)(2,1)S(1)}, u32[]{:S(2)}, u32[]{:S(2)}) collective-permute-start(bf16[218,256]{1,0:T(8,128)(2,1)S(1)} %pooled.1.pool_own), channel_id=1, source_target_pairs={{0,1},{1,2},{2,3},{3,4},{4,5},{5,6},{6,7},{7,8},{8,9},{9,10},{10,1... | collective-permute-start | bytes 334856 | tf_op jit(solution)/shard_map/ppermute | solution.py:56
  60.6 0.0 collective-permute-done.9.refs_3_
  60.6 8.1 %collective-permute-start.3 = (bf16[218,256]{1,0:T(8,128)(2,1)S(1)}, bf16[218,256]{1,0:T(8,128)(2,1)S(1)}, u32[]{:S(2)}, u32[]{:S(2)}) collective-permute-start(bf16[218,256]{1,0:T(8,128)(2,1)S(1)} %pooled.1.pool_own), channel_id=1, source_target_pairs={{1,0},{2,1},{3,2},{4,3},{5,4},{6,5},{7,6},{8,7},{9,8},{10,9},{11,1... | collective-permute-start | bytes 334856 | tf_op jit(solution)/shard_map/ppermute | solution.py:56
  68.7 0.0 collective-permute-done.13.refs_4_
  68.7 0.6 shards_in_order.1.refs_0_
  69.4 0.0 copy-start
  69.4 0.0 copy-start.9
  69.4 0.1 collective-permute-start.14
  69.5 0.0 collective-permute-done.4.per_low
  69.5 3.2 %collective-permute-start.15 = (bf16[8,32,2048]{2,1,0:T(8,128)(2,1)S(1)}, bf16[8,32,2048]{2,1,0:T(8,128)(2,1)S(1)}, u32[]{:S(2)}, u32[]{:S(2)}) collective-permute-start(bf16[8,32,2048]{2,1,0:T(8,128)(2,1)S(1)} %shards_in_order.1.refs_0_), channel_id=1, source_target_pairs={{0,24},{8,0},{16,8},{24,16},{1,25},{9,1},{17,9},{25,17},{2,26},{10... | collective-permute-start | bytes 3145736 | tf_op jit(solution)/shard_map/ppermute | solution.py:333
  72.7 0.0 collective-permute-done.3.pool_high
  72.8 6.8 %embed_qkv.1 = (f32[256,1024]{1,0:T(8,128)S(1)}, bf16[256,1024]{1,0:T(8,128)(2,1)S(1)}, bf16[768,2048]{1,0:T(8,128)(2,1)S(1)}) custom-call(bf16[218,256]{1,0:T(8,128)(2,1)S(1)} %collective-permute-done.2.pool_low, bf16[218,256]{1,0:T(8,128)(2,1)S(1)} %pooled.1.pool_own, bf16[218,256]{1,0:T(8,128)(2,1)S(1)} %collective-permute-done.3.pool_high, ...), custom_call_target="tpu_custom_call" | custom-call | flops 3758096384 | bytes 16777216 | tf_op jit(solution)/shard_map/embed_qkv/pallas_call | solution.py:153
  79.5 11.7 %attention.1 = (f32[256,1024]{1,0:T(8,128)S(1)}, bf16[256,1024]{1,0:T(8,128)(2,1)S(1)}) custom-call(s32[8]{0:T(128)S(1)} %stack.31.place_ref.where_ref, bf16[256,1024]{1,0:T(8,128)(2,1)S(1)} %get-tuple-element.12.query_ref, bf16[768,2048]{1,0:T(8,128)(2,1)S(1)} %get-tuple-element.13.kv_ref, s32[1,256]{1,0:T(1,128)S(1)} %bitcast.20, ...), custom_call_target="tpu_custom_call" | custom-call | flops 1207959552 | bytes 10485760 | tf_op jit(solution)/shard_map/attention/pallas_call | solution.py:220
  91.3 0.1 collective-permute-start.6
  91.4 0.1 collective-permute-start.16
  91.5 0.0 collective-permute-done.14.refs_1_
  91.5 0.1 collective-permute-start.19
  91.7 0.0 copy-start.2
  91.7 3.3 %collective-permute-start.20 = (bf16[4,32,2048]{2,1,0:T(8,128)(2,1)S(1)}, bf16[4,32,2048]{2,1,0:T(8,128)(2,1)S(1)}, u32[]{:S(2)}, u32[]{:S(2)}) collective-permute-start(bf16[4,32,2048]{2,1,0:T(8,128)(2,1)S(1)} %slice.9), channel_id=1, source_target_pairs={{0,24},{8,0},{16,8},{24,16},{1,25},{9,1},{17,9},{25,17},{2,26},{10... | collective-permute-start | bytes 1572872 | tf_op jit(solution)/shard_map/ppermute | solution.py:333
  95.0 2.0 %collective-permute-start.17 = (bf16[8,32,2048]{2,1,0:T(8,128)(2,1)S(1)}, bf16[8,32,2048]{2,1,0:T(8,128)(2,1)S(1)}, u32[]{:S(2)}, u32[]{:S(2)}) collective-permute-start(bf16[8,32,2048]{2,1,0:T(8,128)(2,1)S(1)} %collective-permute-done.14.refs_1_), channel_id=1, source_target_pairs={{0,32},{32,0},{1,33},{33,1},{2,34},{34,2},{3,35},{35,3},{4,36},{36... | collective-permute-start | bytes 3145736 | tf_op jit(solution)/shard_map/ppermute | solution.py:336
  97.0 0.0 collective-permute-done.6.other_ref
  97.0 1.2 collective-permute-start.18
  98.2 8.9 %collective-permute-done.19.refs_6_ = bf16[4,32,2048]{2,1,0:T(8,128)(2,1)S(1)} collective-permute-done((bf16[4,32,2048]{2,1,0:T(8,128)(2,1)S(1)}, bf16[4,32,2048]{2,1,0:T(8,128)(2,1)S(1)}, u32[]{:S(2)}, u32[]{:S(2)}) %collective-permute-start.19) | collective-permute-done | bytes 524320 | tf_op jit(solution)/shard_map/ppermute | solution.py:333
  107.0 1.8 collective-permute-start.21
  108.8 0.0 collective-permute-done.20.refs_7_
  108.8 1.4 collective-permute-start.22
  110.2 7.2 %collective-permute-done.16.refs_3_ = bf16[8,32,2048]{2,1,0:T(8,128)(2,1)S(1)} collective-permute-done((bf16[8,32,2048]{2,1,0:T(8,128)(2,1)S(1)}, bf16[8,32,2048]{2,1,0:T(8,128)(2,1)S(1)}, u32[]{:S(2)}, u32[]{:S(2)}) %collective-permute-start.16) | collective-permute-done | bytes 1048608 | tf_op jit(solution)/shard_map/ppermute | solution.py:336
  117.4 33.2 %collective-permute-done.21.refs_8_ = bf16[4,32,2048]{2,1,0:T(8,128)(2,1)S(1)} collective-permute-done((bf16[4,32,2048]{2,1,0:T(8,128)(2,1)S(1)}, bf16[4,32,2048]{2,1,0:T(8,128)(2,1)S(1)}, u32[]{:S(2)}, u32[]{:S(2)}) %collective-permute-start.21) | collective-permute-done | bytes 524320 | tf_op jit(solution)/shard_map/ppermute | solution.py:336
  150.7 5.7 %mlp_parts.1 = (f32[256,1024]{1,0:T(8,128)S(1)}, f32[256,1024]{1,0:T(8,128)S(1)}) custom-call(s32[8]{0:T(128)S(1)} %stack.31.place_ref.where_ref, bf16[256,1024]{1,0:T(8,128)(2,1)S(1)} %get-tuple-element.16.own_ref, bf16[256,1024]{1,0:T(8,128)(2,1)S(1)} %collective-permute-done.6.other_ref, bf16[8,32,2048]{2,1,0:T(8,128)(2,1)S(1)} %shards_in_order.1.refs_0_, ...), custom_call_target="tpu_custom_call" | custom-call | flops 4294967296 | bytes 12582912 | tf_op jit(solution)/shard_map/mlp_parts/pallas_call | solution.py:316
  156.4 0.0 copy-start.6
  156.4 0.1 collective-permute-start.23
  156.5 2.6 %collective-permute-done.23.other_ref = f32[256,1024]{1,0:T(8,128)S(1)} collective-permute-done((f32[256,1024]{1,0:T(8,128)S(1)}, f32[256,1024]{1,0:T(8,128)S(1)}, u32[]{:S(2)}, u32[]{:S(2)}) %collective-permute-start.23) | collective-permute-done | bytes 1048608 | tf_op jit(solution)/shard_map/ppermute | solution.py:60
  159.2 0.6 final_head.1
  159.8 7.2 %all-gather.1.own_ref = bf16[4,100,256]{2,1,0:T(8,128)(2,1)S(1)} all-gather(bf16[1,100,256]{2,1,0:T(8,128)(2,1)S(1)} %bitcast.15), channel_id=2, replica_groups=mesh['member_hi'=2,'member_core'=2,'node_0'=2,'node_1'=4,'node_2'=8] {'m..., dimensions={0}, use_global_device_ids=true | all-gather | bytes 256000 | tf_op jit(solution)/shard_map/all_gather | solution.py:522
  167.0 1.9 %collective-permute-start.24 = (bf16[4,100,256]{2,1,0:T(8,128)(2,1)S(1)}, bf16[4,100,256]{2,1,0:T(8,128)(2,1)S(1)}, u32[]{:S(2)}, u32[]{:S(2)}) collective-permute-start(bf16[4,100,256]{2,1,0:T(8,128)(2,1)S(1)} %all-gather.1.own_ref), channel_id=1, source_target_pairs={{0,1},{1,2},{2,3},{3,4},{4,5},{5,6},{6,7},{7,8},{8,9},{9,10},{10,1... | collective-permute-start | bytes 614408 | tf_op jit(solution)/shard_map/ppermute | solution.py:56
  168.9 8.1 %collective-permute-start.25 = (bf16[4,100,256]{2,1,0:T(8,128)(2,1)S(1)}, bf16[4,100,256]{2,1,0:T(8,128)(2,1)S(1)}, u32[]{:S(2)}, u32[]{:S(2)}) collective-permute-start(bf16[4,100,256]{2,1,0:T(8,128)(2,1)S(1)} %all-gather.1.own_ref), channel_id=1, source_target_pairs={{1,0},{2,1},{3,2},{4,3},{5,4},{6,5},{7,6},{8,7},{9,8},{10,9},{11,1... | collective-permute-start | bytes 614408 | tf_op jit(solution)/shard_map/ppermute | solution.py:56
  177.0 1.8 decoder_tallies.1.tally_ref
  178.9 1.7 collective-permute-done.24.low_ref
  180.6 1.2 collective-permute-done.25.high_ref
  181.8 2.3 %decoder_crps.1 = f32[1,100,1024]{2,1,0:T(8,128)S(1)} custom-call(s32[8]{0:T(128)S(1)} %stack.31.place_ref.where_ref, bf16[768,1024]{1,0:T(8,128)(2,1)S(1)} %decoder_tallies.1.tally_ref, bf16[218,1024]{1,0:T(8,128)(2,1)S(1)} %copy-done.1, bf16[100,1024]{1,0:T(8,128)(2,1)S(1)} %copy-done.3, bf16[4,100,256]{2,1,0:T(8,128)(2,1)S(1)} %collective-permute-done.24.low_ref, ...), custom_call_target="tpu_custom_call" | custom-call | flops 629145600 | bytes 4194304 | tf_op jit(solution)/shard_map/decoder_crps/pallas_call | solution.py:442
  184.1 1.2 copy.16
  (28 shorter events, 0.1 us)
Async XLA Ops:
  0.0 58.1 %copy-start.1 = (bf16[218,1024]{1,0:T(8,128)(2,1)S(1)}, bf16[218,1024]{1,0:T(8,128)(2,1)}, u32[]{:S(2)}) copy-start(bf16[218,1024]{1,0:T(8,128)(2,1)} %state_ref.1) | copy-start | bytes 1339396
  0.0 58.1 %copy-start.8 = (s32[256]{0:T(256)S(1)}, s32[256]{0:T(256)}, u32[]{:S(2)}) copy-start(s32[256]{0:T(256)} %param.17) | copy-start | bytes 3076
  1.0 9.4 %collective-permute-start.10 = (bf16[32,2048]{1,0:T(8,128)(2,1)S(1)}, bf16[32,2048]{1,0:T(8,128)(2,1)S(1)}, u32[]{:S(2)}, u32[]{:S(2)}) collective-permute-start(bf16[32,2048]{1,0:T(8,128)(2,1)S(1)} %pad_maximum_fusion.refs_0_), channel_id=1, source_target_pairs={{0,1},{1,2},{2,3},{3,4},{4,5},{5,6},{6,7},{7,0},{8,9},{9,10},{10,1... | collective-permute-start | bytes 393224 | tf_op jit(solution)/shard_map/ppermute | solution.py:333
  3.0 16.6 %collective-permute-start.7 = (bf16[32,2048]{1,0:T(8,128)(2,1)S(1)}, bf16[32,2048]{1,0:T(8,128)(2,1)S(1)}, u32[]{:S(2)}, u32[]{:S(2)}) collective-permute-start(bf16[32,2048]{1,0:T(8,128)(2,1)S(1)} %pad_maximum_fusion.refs_0_), channel_id=1, source_target_pairs={{0,7},{1,0},{2,1},{3,2},{4,3},{5,4},{6,5},{7,6},{8,15},{9,8},{10,9... | collective-permute-start | bytes 393224 | tf_op jit(solution)/shard_map/ppermute | solution.py:333
  7.0 43.6 %collective-permute-start = (bf16[218,1024]{1,0:T(8,128)(2,1)}, bf16[218,1024]{1,0:T(8,128)(2,1)S(1)}, u32[]{:S(2)}, u32[]{:S(2)}) collective-permute-start(bf16[218,1024]{1,0:T(8,128)(2,1)} %state_ref.1), channel_id=1, source_target_pairs={{0,1},{1,2},{2,3},{3,4},{4,5},{5,6},{6,7},{7,8},{8,9},{9,10},{10,1... | collective-permute-start | bytes 1339400 | tf_op jit(solution)/shard_map/ppermute | solution.py:56
  10.4 17.3 %collective-permute-start.11 = (bf16[32,2048]{1,0:T(8,128)(2,1)S(1)}, bf16[32,2048]{1,0:T(8,128)(2,1)S(1)}, u32[]{:S(2)}, u32[]{:S(2)}) collective-permute-start(bf16[32,2048]{1,0:T(8,128)(2,1)S(1)} %collective-permute-done.10.refs_7_), channel_id=1, source_target_pairs={{0,1},{1,2},{2,3},{3,4},{4,5},{5,6},{6,7},{7,0},{8,9},{9,10},{10,1... | collective-permute-start | bytes 393224 | tf_op jit(solution)/shard_map/ppermute | solution.py:333
  10.4 47.7 %collective-permute-start.1 = (bf16[218,1024]{1,0:T(8,128)(2,1)}, bf16[218,1024]{1,0:T(8,128)(2,1)S(1)}, u32[]{:S(2)}, u32[]{:S(2)}) collective-permute-start(bf16[218,1024]{1,0:T(8,128)(2,1)} %state_ref.1), channel_id=1, source_target_pairs={{1,0},{2,1},{3,2},{4,3},{5,4},{6,5},{7,6},{8,7},{9,8},{10,9},{11,1... | collective-permute-start | bytes 1339400 | tf_op jit(solution)/shard_map/ppermute | solution.py:56
  17.6 51.9 %collective-permute-start.4 = (bf16[256,1024]{1,0:T(8,128)(2,1)}, bf16[256,1024]{1,0:T(8,128)(2,1)S(1)}, u32[]{:S(2)}, u32[]{:S(2)}) collective-permute-start(bf16[256,1024]{1,0:T(8,128)(2,1)} %bitcast.21), channel_id=1, source_target_pairs={{0,1},{1,2},{2,3},{3,4},{4,5},{5,6},{6,7},{7,8},{8,9},{9,10},{10,1... | collective-permute-start | bytes 1572872 | tf_op jit(solution)/shard_map/ppermute | solution.py:56
  19.6 53.2 %collective-permute-start.5 = (bf16[256,1024]{1,0:T(8,128)(2,1)}, bf16[256,1024]{1,0:T(8,128)(2,1)S(1)}, u32[]{:S(2)}, u32[]{:S(2)}) collective-permute-start(bf16[256,1024]{1,0:T(8,128)(2,1)} %bitcast.22), channel_id=1, source_target_pairs={{1,0},{2,1},{3,2},{4,3},{5,4},{6,5},{7,6},{8,7},{9,8},{10,9},{11,1... | collective-permute-start | bytes 1572872 | tf_op jit(solution)/shard_map/ppermute | solution.py:56
  27.7 13.1 %collective-permute-start.8 = (bf16[32,2048]{1,0:T(8,128)(2,1)S(1)}, bf16[32,2048]{1,0:T(8,128)(2,1)S(1)}, u32[]{:S(2)}, u32[]{:S(2)}) collective-permute-start(bf16[32,2048]{1,0:T(8,128)(2,1)S(1)} %collective-permute-done.7.refs_1_), channel_id=1, source_target_pairs={{0,7},{1,0},{2,1},{3,2},{4,3},{5,4},{6,5},{7,6},{8,15},{9,8},{10,9... | collective-permute-start | bytes 393224 | tf_op jit(solution)/shard_map/ppermute | solution.py:333
  40.8 6.6 %collective-permute-start.12 = (bf16[32,2048]{1,0:T(8,128)(2,1)S(1)}, bf16[32,2048]{1,0:T(8,128)(2,1)S(1)}, u32[]{:S(2)}, u32[]{:S(2)}) collective-permute-start(bf16[32,2048]{1,0:T(8,128)(2,1)S(1)} %collective-permute-done.11.refs_6_), channel_id=1, source_target_pairs={{0,1},{1,2},{2,3},{3,4},{4,5},{5,6},{6,7},{7,0},{8,9},{9,10},{10,1... | collective-permute-start | bytes 393224 | tf_op jit(solution)/shard_map/ppermute | solution.py:333
  47.4 13.1 %collective-permute-start.9 = (bf16[32,2048]{1,0:T(8,128)(2,1)S(1)}, bf16[32,2048]{1,0:T(8,128)(2,1)S(1)}, u32[]{:S(2)}, u32[]{:S(2)}) collective-permute-start(bf16[32,2048]{1,0:T(8,128)(2,1)S(1)} %collective-permute-done.8.refs_2_), channel_id=1, source_target_pairs={{0,7},{1,0},{2,1},{3,2},{4,3},{5,4},{6,5},{7,6},{8,15},{9,8},{10,9... | collective-permute-start | bytes 393224 | tf_op jit(solution)/shard_map/ppermute | solution.py:333
  50.6 18.2 %collective-permute-start.13 = (bf16[32,2048]{1,0:T(8,128)(2,1)S(1)}, bf16[32,2048]{1,0:T(8,128)(2,1)S(1)}, u32[]{:S(2)}, u32[]{:S(2)}) collective-permute-start(bf16[32,2048]{1,0:T(8,128)(2,1)S(1)} %collective-permute-done.12.refs_5_), channel_id=1, source_target_pairs={{0,1},{1,2},{2,3},{3,4},{4,5},{5,6},{6,7},{7,0},{8,9},{9,10},{10,1... | collective-permute-start | bytes 393224 | tf_op jit(solution)/shard_map/ppermute | solution.py:333
  50.6 0.7 copy-start.5
  51.4 0.7 copy-start.7
  58.0 14.7 %copy-start.4 = (f32[3,1024]{1,0:T(4,128)S(1)}, f32[3,1024]{1,0:T(4,128)}, u32[]{:S(2)}) copy-start(f32[3,1024]{1,0:T(4,128)} %gain_ref.5) | copy-start | bytes 36868
  58.0 14.7 %copy-start.10 = (bf16[1,256,1024]{2,1,0:T(8,128)(2,1)S(1)}, bf16[1,256,1024]{2,1,0:T(8,128)(2,1)}, u32[]{:S(2)}) copy-start(bf16[1,256,1024]{2,1,0:T(8,128)(2,1)} %param.20) | copy-start | bytes 1572868
  58.1 14.7 %copy-start.11 = (bf16[218,1024]{1,0:T(8,128)(2,1)S(1)}, bf16[218,1024]{1,0:T(8,128)(2,1)}, u32[]{:S(2)}) copy-start(bf16[218,1024]{1,0:T(8,128)(2,1)} %embed_ref.1) | copy-start | bytes 1339396
  58.6 14.1 %collective-permute-start.2 = (bf16[218,256]{1,0:T(8,128)(2,1)S(1)}, bf16[218,256]{1,0:T(8,128)(2,1)S(1)}, u32[]{:S(2)}, u32[]{:S(2)}) collective-permute-start(bf16[218,256]{1,0:T(8,128)(2,1)S(1)} %pooled.1.pool_own), channel_id=1, source_target_pairs={{0,1},{1,2},{2,3},{3,4},{4,5},{5,6},{6,7},{7,8},{8,9},{9,10},{10,1... | collective-permute-start | bytes 334856 | tf_op jit(solution)/shard_map/ppermute | solution.py:56
  60.6 12.1 %collective-permute-start.3 = (bf16[218,256]{1,0:T(8,128)(2,1)S(1)}, bf16[218,256]{1,0:T(8,128)(2,1)S(1)}, u32[]{:S(2)}, u32[]{:S(2)}) collective-permute-start(bf16[218,256]{1,0:T(8,128)(2,1)S(1)} %pooled.1.pool_own), channel_id=1, source_target_pairs={{1,0},{2,1},{3,2},{4,3},{5,4},{6,5},{7,6},{8,7},{9,8},{10,9},{11,1... | collective-permute-start | bytes 334856 | tf_op jit(solution)/shard_map/ppermute | solution.py:56
  69.4 10.2 %copy-start = (bf16[1024,1024]{1,0:T(8,128)(2,1)S(1)}, bf16[1024,1024]{1,0:T(8,128)(2,1)}, u32[]{:S(2)}) copy-start(bf16[1024,1024]{1,0:T(8,128)(2,1)} %out_hbm.1) | copy-start | bytes 6291460
  69.4 10.2 %copy-start.9 = (s32[256]{0:T(256)S(1)}, s32[256]{0:T(256)}, u32[]{:S(2)}) copy-start(s32[256]{0:T(256)} %param.18) | copy-start | bytes 3076
  69.4 22.1 %collective-permute-start.14 = (bf16[8,32,2048]{2,1,0:T(8,128)(2,1)S(1)}, bf16[8,32,2048]{2,1,0:T(8,128)(2,1)S(1)}, u32[]{:S(2)}, u32[]{:S(2)}) collective-permute-start(bf16[8,32,2048]{2,1,0:T(8,128)(2,1)S(1)} %shards_in_order.1.refs_0_), channel_id=1, source_target_pairs={{0,8},{8,16},{16,24},{24,0},{1,9},{9,17},{17,25},{25,1},{2,10},{10... | collective-permute-start | bytes 3145736 | tf_op jit(solution)/shard_map/ppermute | solution.py:333
  69.5 22.1 %collective-permute-start.15 = (bf16[8,32,2048]{2,1,0:T(8,128)(2,1)S(1)}, bf16[8,32,2048]{2,1,0:T(8,128)(2,1)S(1)}, u32[]{:S(2)}, u32[]{:S(2)}) collective-permute-start(bf16[8,32,2048]{2,1,0:T(8,128)(2,1)S(1)} %shards_in_order.1.refs_0_), channel_id=1, source_target_pairs={{0,24},{8,0},{16,8},{24,16},{1,25},{9,1},{17,9},{25,17},{2,26},{10... | collective-permute-start | bytes 3145736 | tf_op jit(solution)/shard_map/ppermute | solution.py:333
  91.3 5.7 %collective-permute-start.6 = (bf16[256,1024]{1,0:T(8,128)(2,1)S(1)}, bf16[256,1024]{1,0:T(8,128)(2,1)S(1)}, u32[]{:S(2)}, u32[]{:S(2)}) collective-permute-start(bf16[256,1024]{1,0:T(8,128)(2,1)S(1)} %get-tuple-element.16.own_ref), channel_id=1, source_target_pairs={{0,64},{64,0},{1,65},{65,1},{2,66},{66,2},{3,67},{67,3},{4,68},{68... | collective-permute-start | bytes 1572872 | tf_op jit(solution)/shard_map/ppermute | solution.py:60
  91.4 26.1 %collective-permute-start.16 = (bf16[8,32,2048]{2,1,0:T(8,128)(2,1)S(1)}, bf16[8,32,2048]{2,1,0:T(8,128)(2,1)S(1)}, u32[]{:S(2)}, u32[]{:S(2)}) collective-permute-start(bf16[8,32,2048]{2,1,0:T(8,128)(2,1)S(1)} %shards_in_order.1.refs_0_), channel_id=1, source_target_pairs={{0,32},{32,0},{1,33},{33,1},{2,34},{34,2},{3,35},{35,3},{4,36},{36... | collective-permute-start | bytes 3145736 | tf_op jit(solution)/shard_map/ppermute | solution.py:336
  91.5 15.5 %collective-permute-start.19 = (bf16[4,32,2048]{2,1,0:T(8,128)(2,1)S(1)}, bf16[4,32,2048]{2,1,0:T(8,128)(2,1)S(1)}, u32[]{:S(2)}, u32[]{:S(2)}) collective-permute-start(bf16[4,32,2048]{2,1,0:T(8,128)(2,1)S(1)} %slice.8), channel_id=1, source_target_pairs={{0,8},{8,16},{16,24},{24,0},{1,9},{9,17},{17,25},{25,1},{2,10},{10... | collective-permute-start | bytes 1572872 | tf_op jit(solution)/shard_map/ppermute | solution.py:333
  91.7 67.5 %copy-start.2 = (bf16[1024,100]{0,1:T(8,128)(2,1)S(1)}, bf16[1024,100]{0,1:T(8,128)(2,1)}, u32[]{:S(2)}) copy-start(bf16[1024,100]{0,1:T(8,128)(2,1)} %param.27) | copy-start | bytes 614404
  91.7 17.1 %collective-permute-start.20 = (bf16[4,32,2048]{2,1,0:T(8,128)(2,1)S(1)}, bf16[4,32,2048]{2,1,0:T(8,128)(2,1)S(1)}, u32[]{:S(2)}, u32[]{:S(2)}) collective-permute-start(bf16[4,32,2048]{2,1,0:T(8,128)(2,1)S(1)} %slice.9), channel_id=1, source_target_pairs={{0,24},{8,0},{16,8},{24,16},{1,25},{9,1},{17,9},{25,17},{2,26},{10... | collective-permute-start | bytes 1572872 | tf_op jit(solution)/shard_map/ppermute | solution.py:333
  95.0 55.6 %collective-permute-start.17 = (bf16[8,32,2048]{2,1,0:T(8,128)(2,1)S(1)}, bf16[8,32,2048]{2,1,0:T(8,128)(2,1)S(1)}, u32[]{:S(2)}, u32[]{:S(2)}) collective-permute-start(bf16[8,32,2048]{2,1,0:T(8,128)(2,1)S(1)} %collective-permute-done.14.refs_1_), channel_id=1, source_target_pairs={{0,32},{32,0},{1,33},{33,1},{2,34},{34,2},{3,35},{35,3},{4,36},{36... | collective-permute-start | bytes 3145736 | tf_op jit(solution)/shard_map/ppermute | solution.py:336
  97.0 53.7 %collective-permute-start.18 = (bf16[8,32,2048]{2,1,0:T(8,128)(2,1)S(1)}, bf16[8,32,2048]{2,1,0:T(8,128)(2,1)S(1)}, u32[]{:S(2)}, u32[]{:S(2)}) collective-permute-start(bf16[8,32,2048]{2,1,0:T(8,128)(2,1)S(1)} %collective-permute-done.15.refs_2_), channel_id=1, source_target_pairs={{0,160},{160,0},{32,128},{128,32},{1,161},{161,1},{33,129},{129,33... | collective-permute-start | bytes 3145736 | tf_op jit(solution)/shard_map/ppermute | solution.py:339
  107.0 43.6 %collective-permute-start.21 = (bf16[4,32,2048]{2,1,0:T(8,128)(2,1)S(1)}, bf16[4,32,2048]{2,1,0:T(8,128)(2,1)S(1)}, u32[]{:S(2)}, u32[]{:S(2)}) collective-permute-start(bf16[4,32,2048]{2,1,0:T(8,128)(2,1)S(1)} %collective-permute-done.19.refs_6_), channel_id=1, source_target_pairs={{0,32},{32,0},{1,33},{33,1},{2,34},{34,2},{3,35},{35,3},{4,36},{36... | collective-permute-start | bytes 1572872 | tf_op jit(solution)/shard_map/ppermute | solution.py:336
  108.8 41.9 %collective-permute-start.22 = (bf16[4,32,2048]{2,1,0:T(8,128)(2,1)S(1)}, bf16[4,32,2048]{2,1,0:T(8,128)(2,1)S(1)}, u32[]{:S(2)}, u32[]{:S(2)}) collective-permute-start(bf16[4,32,2048]{2,1,0:T(8,128)(2,1)S(1)} %collective-permute-done.20.refs_7_), channel_id=1, source_target_pairs={{0,160},{160,0},{32,128},{128,32},{1,161},{161,1},{33,129},{129,33... | collective-permute-start | bytes 1572872 | tf_op jit(solution)/shard_map/ppermute | solution.py:339
  156.4 20.6 %copy-start.6 = (s32[1024,4]{0,1:T(4,128)S(1)}, s32[1024,4]{0,1:T(4,128)}, u32[]{:S(2)}) copy-start(s32[1024,4]{0,1:T(4,128)} %param.19) | copy-start | bytes 49156
  156.4 2.7 %collective-permute-start.23 = (f32[256,1024]{1,0:T(8,128)S(1)}, f32[256,1024]{1,0:T(8,128)S(1)}, u32[]{:S(2)}, u32[]{:S(2)}) collective-permute-start(f32[256,1024]{1,0:T(8,128)S(1)} %get-tuple-element.18), channel_id=1, source_target_pairs={{0,64},{64,0},{1,65},{65,1},{2,66},{66,2},{3,67},{67,3},{4,68},{68... | collective-permute-start | bytes 3145736 | tf_op jit(solution)/shard_map/ppermute | solution.py:60
  159.2 22.6 %copy-start.3 = (bf16[100,1024]{1,0:T(8,128)(2,1)S(1)}, bf16[100,1024]{1,0:T(8,128)(2,1)}, u32[]{:S(2)}) copy-start(bf16[100,1024]{1,0:T(8,128)(2,1)} %truth_ref.1) | copy-start | bytes 614404
  167.0 13.6 %collective-permute-start.24 = (bf16[4,100,256]{2,1,0:T(8,128)(2,1)S(1)}, bf16[4,100,256]{2,1,0:T(8,128)(2,1)S(1)}, u32[]{:S(2)}, u32[]{:S(2)}) collective-permute-start(bf16[4,100,256]{2,1,0:T(8,128)(2,1)S(1)} %all-gather.1.own_ref), channel_id=1, source_target_pairs={{0,1},{1,2},{2,3},{3,4},{4,5},{5,6},{6,7},{7,8},{8,9},{9,10},{10,1... | collective-permute-start | bytes 614408 | tf_op jit(solution)/shard_map/ppermute | solution.py:56
  168.9 12.9 %collective-permute-start.25 = (bf16[4,100,256]{2,1,0:T(8,128)(2,1)S(1)}, bf16[4,100,256]{2,1,0:T(8,128)(2,1)S(1)}, u32[]{:S(2)}, u32[]{:S(2)}) collective-permute-start(bf16[4,100,256]{2,1,0:T(8,128)(2,1)S(1)} %all-gather.1.own_ref), channel_id=1, source_target_pairs={{1,0},{2,1},{3,2},{4,3},{5,4},{6,5},{7,6},{8,7},{9,8},{10,9},{11,1... | collective-permute-start | bytes 614408 | tf_op jit(solution)/shard_map/ppermute | solution.py:56
